TPU v7x, 1024 devices: a whole 8x8x8 slice. The times are simulated.
1024 devices in a mesh: pipe: 8 (over z), ctx: 16 (over x, core), head: 8 (over y).
Axes of the slice: x: 8, y: 8, z: 8, core: 2. Of those that a mesh axis runs over, the one named last changes fastest.
Arguments:
- queries: bfloat16 [8, 2048, 8192], P('pipe', 'ctx', 'head'), may hold values from -6 to 6
- key_states: bfloat16 [8, 2048, 1024], P('pipe', 'ctx', 'head'), may hold values from -6 to 6
- value_states: bfloat16 [8, 2048, 1024], P('pipe', 'ctx', 'head'), may hold values from -6 to 6
- upstream: bfloat16 [8, 2048, 8192], P('pipe', ('ctx', 'head')), may hold values from -6 to 6
- selected: int32 [8, 8, 32, 8], P('pipe', 'head', 'ctx'), may hold values from 0 to 31, as said below
Outputs:
- query_grad: bfloat16 [8, 2048, 8192], P('pipe', 'ctx', 'head')
- key_grad: bfloat16 [8, 2048, 1024], P('pipe', 'ctx', 'head')
- value_grad: bfloat16 [8, 2048, 1024], P('pipe', 'ctx', 'head')
Inputs may be any that keep to these rules, and one draw needn't show every extreme that they name: `selected`: for query block b, entry 0 is b; the other 7 entries are distinct; min(b, 7) of them name blocks before b, the rest name blocks after b.
All inputs are finite; a program needn't handle non-finite values.
Results may differ from a plain program's by a relative error of at most 0.015.
Values may be sent and summed in bfloat16 or wider, within the bound.
A program may use at most 32 MiB of HBM per device.

v0:
```python
import jax
import jax.numpy as jnp
from jax import lax
from jax.sharding import PartitionSpec as P

HD = 128
BLK = 64
TOPB = 8
GROUP = 8


def shifted_2(value, axis, steps):
    count = lax.axis_size(axis)
    pairs = [(source, (source + steps) % count) for source in range(count)]
    return lax.ppermute(value, axis, pairs)


def per_device(queries, key_states, value_states, upstream, selected):
    arrived = shifted_2(upstream, "pipe", -1)
    out_grad = lax.all_to_all(arrived, "head", split_axis=2, concat_axis=1, tiled=True)
    whole_keys, whole_values = (
        lax.all_gather(key_states, "ctx", axis=1, tiled=True),
        lax.all_gather(value_states, "ctx", axis=1, tiled=True),
    )
    tokens = whole_keys.shape[1]
    tok_dev = queries.shape[1]
    local_heads = key_states.shape[2] // HD
    local_blocks = tok_dev // BLK
    first_block = lax.axis_index("ctx") * local_blocks
    score_scale = HD ** (-0.5)
    key_table = whole_keys[0].reshape(tokens, local_heads, HD)
    value_table = whole_values[0].reshape(tokens, local_heads, HD)
    query_tiles = queries[0].reshape(local_blocks, BLK, local_heads, GROUP, HD)
    grad_tiles = out_grad[0].reshape(local_blocks, BLK, local_heads, GROUP, HD)
    chosen = jnp.transpose(selected[0], (1, 0, 2))
    block_ids = first_block + jnp.arange(local_blocks, dtype=jnp.int32)
    offsets = jnp.arange(BLK, dtype=jnp.int32)
    head_index = jnp.arange(local_heads, dtype=jnp.int32)[:, None]

    def block_step(running, inputs):
        key_sums, value_sums = running
        query_blk, grad_blk, chosen_blk, block_index = inputs
        row_index = (chosen_blk[:, :, None] * BLK + offsets).reshape(local_heads, TOPB * BLK)
        key_rows = key_table[row_index, head_index]
        value_rows = value_table[row_index, head_index]
        scores = (
            jnp.einsum("icgh,cjh->cgij", query_blk, key_rows, preferred_element_type=jnp.float32)
            * score_scale
        )
        query_pos = block_index * BLK + offsets
        visible = row_index[:, None, None, :] <= query_pos[None, None, :, None]
        scores = jnp.where(visible, scores, -jnp.inf)
        row_max = jnp.max(scores, axis=-1, keepdims=True)
        shifted = jnp.exp(scores - row_max)
        weights = shifted / jnp.sum(shifted, axis=-1, keepdims=True)
        weight_grad = jnp.einsum(
            "icgh,cjh->cgij", grad_blk, value_rows, preferred_element_type=jnp.float32
        )
        row_delta = jnp.sum(weights * weight_grad, axis=-1, keepdims=True)
        score_grad = (weights * (weight_grad - row_delta) * score_scale).astype(jnp.bfloat16)
        weight_half = weights.astype(jnp.bfloat16)
        query_part = jnp.einsum(
            "cgij,cjh->icgh", score_grad, key_rows, preferred_element_type=jnp.float32
        )
        key_part = jnp.einsum(
            "cgij,icgh->cjh", score_grad, query_blk, preferred_element_type=jnp.float32
        )
        value_part = jnp.einsum(
            "cgij,icgh->cjh", weight_half, grad_blk, preferred_element_type=jnp.float32
        )
        key_sums = key_sums.at[row_index, head_index].add(key_part)
        value_sums = value_sums.at[row_index, head_index].add(value_part)
        return ((key_sums, value_sums), query_part.astype(jnp.bfloat16))

    start = (
        jnp.zeros((tokens, local_heads, HD), jnp.float32),
        jnp.zeros((tokens, local_heads, HD), jnp.float32),
    )
    (key_sums, value_sums), query_parts = lax.scan(
        block_step, start, (query_tiles, grad_tiles, chosen, block_ids)
    )
    key_flat = key_sums.reshape(tokens, local_heads * HD)
    value_flat = value_sums.reshape(tokens, local_heads * HD)
    summed = lax.psum_scatter(
        jnp.concatenate([key_flat, value_flat], axis=1).astype(jnp.bfloat16),
        "ctx",
        scatter_dimension=0,
        tiled=True,
    ).astype(jnp.float32)
    half_width = local_heads * HD
    query_grad = query_parts.reshape(1, tok_dev, local_heads * GROUP * HD)
    key_grad = summed[:, :half_width].astype(jnp.bfloat16)[None]
    value_grad = summed[:, half_width:].astype(jnp.bfloat16)[None]
    return (query_grad, key_grad, value_grad)


def solution(mesh):
    placed = (
        P("pipe", "ctx", "head"),
        P("pipe", "ctx", "head"),
        P("pipe", "ctx", "head"),
        P("pipe", ("ctx", "head"), None),
        P("pipe", "head", "ctx", None),
    )
    return jax.shard_map(
        per_device,
        mesh=mesh,
        in_specs=placed,
        out_specs=(P("pipe", "ctx", "head"), P("pipe", "ctx", "head"), P("pipe", "ctx", "head")),
        check_vma=False,
    )
```

profile of v0, /device:TPU:1, one launch (start us, length us, event | category | flops | bytes accessed | tf_op | source)
XLA Modules:
  0.0 274.9 jit_solution(15529032836053602397)
XLA Ops:
  7.2 17.9 %collective-permute-start = (bf16[1,16,8192]{2,1,0:T(8,128)(2,1)}, bf16[1,16,8192]{2,1,0:T(8,128)(2,1)S(1)}, u32[]{:S(2)}, u32[]{:S(2)}) collective-permute-start(bf16[1,16,8192]{2,1,0:T(8,128)(2,1)} %param.10), channel_id=1, source_target_pairs={{0,896},{128,0},{256,128},{384,256},{512,384},{640,512},{768,640},... | collective-permute-start | bytes 786440 | tf_op jit(solution)/shard_map/ppermute | solution.py:15
  25.0 1.7 copy.39
  27.3 3.0 %collective-permute-done = bf16[1,16,8192]{2,1,0:T(8,128)(2,1)S(1)} collective-permute-done((bf16[1,16,8192]{2,1,0:T(8,128)(2,1)}, bf16[1,16,8192]{2,1,0:T(8,128)(2,1)S(1)}, u32[]{:S(2)}, u32[]{:S(2)}) %collective-permute-start) | collective-permute-done | bytes 262176 | tf_op jit(solution)/shard_map/ppermute | solution.py:15
  30.3 6.6 %copy.28 = bf16[1,16,8192]{1,0,2:T(2,128)(2,1)} copy(bf16[1,16,8192]{2,1,0:T(8,128)(2,1)S(1)} %collective-permute-done) | data formatting | bytes 524288 | tf_op jit(solution)/shard_map/ppermute | solution.py:15
  37.4 45.2 %reduce.9 = bf16[8192,16]{1,0:T(8,128)(2,1)S(1)} reduce(bf16[8192,1,16]{2,1,0:T(2,128)(2,1)} %bitcast.154, bf16[]{:T(256)} %broadcast.163), dimensions={1}, to_apply=%bitcast.87.reduce_sub_computation | reduce | bytes 524290
  82.7 2.8 %reshape.280 = bf16[8,2,8192]{2,1,0:T(2,128)(2,1)} reshape(bf16[8192,16]{1,0:T(8,128)(2,1)S(1)} %reduce.9) | data formatting | bytes 524288
  85.5 7.3 %all-to-all-start = ((bf16[8,2,8192]{2,1,0:T(2,128)(2,1)}), bf16[8,2,8192]{2,1,0:T(2,128)(2,1)S(1)}, u32[]{:S(2)}, u32[]{:S(2)}) async-start(bf16[8,2,8192]{2,1,0:T(2,128)(2,1)} %reshape.280), calls=%async_computation | async-start | bytes 524288 | tf_op jit(solution)/shard_map/all_to_all | solution.py:20
  92.8 20.1 %all_gather.6 = bf16[1,2048,128]{2,1,0:T(8,128)(2,1)S(1)} all-gather(bf16[1,128,128]{2,1,0:T(8,128)(2,1)S(1)} %copy-done.7), channel_id=1, replica_groups=mesh['pipe'=8,'ctx'=16,'head'=8] {'ctx'}, dimensions={1}, use_global_device_ids=true | all-gather | bytes 557056 | tf_op jit(solution)/shard_map/all_gather | solution.py:22
  112.9 18.2 %all_gather.7 = bf16[1,2048,128]{2,1,0:T(8,128)(2,1)} all-gather(bf16[1,128,128]{2,1,0:T(8,128)(2,1)S(1)} %copy-done.8), channel_id=1, replica_groups=mesh['pipe'=8,'ctx'=16,'head'=8] {'ctx'}, dimensions={1}, use_global_device_ids=true | all-gather | bytes 557056 | tf_op jit(solution)/shard_map/all_gather | solution.py:23
  131.1 5.1 %reshape.281 = bf16[8192,1,16]{2,1,0:T(2,128)(2,1)} reshape(bf16[8,2,8192]{2,1,0:T(2,128)(2,1)S(1)} %all-to-all-done) | data formatting | bytes 524288
  136.2 7.9 %copy.29 = bf16[1,16,8192]{2,1,0:T(8,128)(2,1)S(1)} copy(bf16[1,16,8192]{1,0,2:T(2,128)(2,1)} %bitcast.155) | data formatting | bytes 524288 | tf_op jit(solution)/shard_map/all_to_all | solution.py:20
  145.3 61.2 %while.16 = (s32[]{:T(128)}, f32[2048,1,128]{2,0,1:T(8,128)S(1)}, f32[2048,1,128]{2,0,1:T(8,128)S(1)}, bf16[2,64,1,8,128]{4,3,1,0,2:T(8,128)(2,1)}, s32[2,1,8]{2...) while((s32[]{:T(128)}, f32[2048,1,128]{2,0,1:T(8,128)S(1)}, ...), condition=%wide.region_6.7_spmd.clone.clone, body=%wide.region_0.6_spmd.clone.clone.sunk | while | flops 340496960 | bytes 24007620 | solution.py:79
  146.3 1.2 dynamic_slice.35
  149.1 2.5 gather_fusion
  152.6 1.1 fusion.33
  154.1 1.3 convolution_bitcast_fusion.6
  155.4 4.1 %scatter_fusion.1 = f32[2048,128]{1,0:T(8,128)S(1)} fusion(f32[2048,128]{1,0:T(8,128)S(1)} %bitcast.150, s32[512]{0:T(512)S(1)} %bitcast.159, f32[512,128]{1,0:T(8,128)} %convolution_bitcast_fusion.6), kind=kCustom, calls=%fused_computation.3.clone.clone.1 | custom fusion | flops 65536 | bytes 788480 | tf_op jit(solution)/shard_map/while/body/eval_jaxpr/scatter-add | solution.py:72
  159.5 8.3 %gather_fusion.1 = bf16[512,128]{1,0:T(8,128)(2,1)} fusion(bf16[2048,1,128]{2,0,1:T(8,128)(2,1)} %get-tuple-element.311, s32[512]{0:T(512)S(1)} %bitcast.147), kind=kCustom, calls=%fused_computation.1.clone.clone.1 | custom fusion | bytes 266240 | tf_op jit(solution)/shard_map/while/body/eval_jaxpr/gather | solution.py:45
  167.8 1.3 multiply_reduce_fusion.2
  169.5 1.1 convolution_bitcast_fusion.5
  170.6 4.2 %scatter_fusion = f32[2048,128]{1,0:T(8,128)S(1)} fusion(f32[2048,128]{1,0:T(8,128)S(1)} %bitcast.148, s32[512]{0:T(512)S(1)} %bitcast.160, f32[512,128]{1,0:T(8,128)} %convolution_bitcast_fusion.5), kind=kCustom, calls=%fused_computation.2.clone.clone.1 | custom fusion | flops 65536 | bytes 788480 | tf_op jit(solution)/shard_map/while/body/eval_jaxpr/scatter-add | solution.py:71
  176.9 1.2 dynamic_slice.35
  179.7 2.5 gather_fusion
  183.2 1.1 fusion.33
  184.7 1.3 convolution_bitcast_fusion.6
  186.0 4.1 %scatter_fusion.1 = f32[2048,128]{1,0:T(8,128)S(1)} fusion(f32[2048,128]{1,0:T(8,128)S(1)} %bitcast.150, s32[512]{0:T(512)S(1)} %bitcast.159, f32[512,128]{1,0:T(8,128)} %convolution_bitcast_fusion.6), kind=kCustom, calls=%fused_computation.3.clone.clone.1 | custom fusion | flops 65536 | bytes 788480 | tf_op jit(solution)/shard_map/while/body/eval_jaxpr/scatter-add | solution.py:72
  190.1 8.4 %gather_fusion.1 = bf16[512,128]{1,0:T(8,128)(2,1)} fusion(bf16[2048,1,128]{2,0,1:T(8,128)(2,1)} %get-tuple-element.311, s32[512]{0:T(512)S(1)} %bitcast.147), kind=kCustom, calls=%fused_computation.1.clone.clone.1 | custom fusion | bytes 266240 | tf_op jit(solution)/shard_map/while/body/eval_jaxpr/gather | solution.py:45
  198.4 1.3 multiply_reduce_fusion.2
  201.2 4.2 %scatter_fusion = f32[2048,128]{1,0:T(8,128)S(1)} fusion(f32[2048,128]{1,0:T(8,128)S(1)} %bitcast.148, s32[512]{0:T(512)S(1)} %bitcast.160, f32[512,128]{1,0:T(8,128)} %convolution_bitcast_fusion.5), kind=kCustom, calls=%fused_computation.2.clone.clone.1 | custom fusion | flops 65536 | bytes 788480 | tf_op jit(solution)/shard_map/while/body/eval_jaxpr/scatter-add | solution.py:71
  206.7 1.1 pad_maximum_fusion
  208.7 58.0 %reduce-scatter.2.cloned.1.call-done = bf16[128,256]{1,0:T(8,128)(2,1)} async-done(((bf16[2048,256]{1,0:T(8,128)(2,1)}), bf16[128,256]{1,0:T(8,128)(2,1)}) %reduce-scatter.2.cloned.1.call-update) | async-done | bytes 65552 | tf_op jit(solution)/shard_map/reduce_scatter | solution.py:84
  266.7 1.4 slice_bitcast_fusion
  (83 shorter events, 13.8 us)
Async XLA Ops:
  7.2 23.1 %collective-permute-start = (bf16[1,16,8192]{2,1,0:T(8,128)(2,1)}, bf16[1,16,8192]{2,1,0:T(8,128)(2,1)S(1)}, u32[]{:S(2)}, u32[]{:S(2)}) collective-permute-start(bf16[1,16,8192]{2,1,0:T(8,128)(2,1)} %param.10), channel_id=1, source_target_pairs={{0,896},{128,0},{256,128},{384,256},{512,384},{640,512},{768,640},... | collective-permute-start | bytes 786440 | tf_op jit(solution)/shard_map/ppermute | solution.py:15
  82.7 10.2 %copy-start.7 = (bf16[1,128,128]{2,1,0:T(8,128)(2,1)S(1)}, bf16[1,128,128]{2,1,0:T(8,128)(2,1)}, u32[]{:S(2)}) copy-start(bf16[1,128,128]{2,1,0:T(8,128)(2,1)} %param.8) | copy-start | bytes 98308
  82.7 30.3 %copy-start.8 = (bf16[1,128,128]{2,1,0:T(8,128)(2,1)S(1)}, bf16[1,128,128]{2,1,0:T(8,128)(2,1)}, u32[]{:S(2)}) copy-start(bf16[1,128,128]{2,1,0:T(8,128)(2,1)} %param.9) | copy-start | bytes 98308
  85.5 45.6 %all-to-all-start = ((bf16[8,2,8192]{2,1,0:T(2,128)(2,1)}), bf16[8,2,8192]{2,1,0:T(2,128)(2,1)S(1)}, u32[]{:S(2)}, u32[]{:S(2)}) async-start(bf16[8,2,8192]{2,1,0:T(2,128)(2,1)} %reshape.280), calls=%async_computation | async-start | bytes 524288 | tf_op jit(solution)/shard_map/all_to_all | solution.py:20
  92.8 173.9 %reduce-scatter.2.cloned.1.call-start = ((), (), s32[]{:S(2)}) async-start(), calls=%async_computation.2 | async-start | bytes 1114112 | tf_op jit(solution)/shard_map/reduce_scatter | solution.py:84
  145.3 7.3 %copy-start = (bf16[2048,1,128]{2,0,1:T(8,128)(2,1)}, bf16[2048,1,128]{2,0,1:T(8,128)(2,1)S(1)}, u32[]{:S(2)}) copy-start(bf16[2048,1,128]{2,0,1:T(8,128)(2,1)S(1)} %get-tuple-element.309) | copy-start | bytes 1572868 | tf_op jit(solution)/shard_map/while
  169.5 1.1 copy-start.2
  170.6 4.2 %copy-start.3 = (bf16[8,64,512]{2,1,0:T(8,128)(2,1)S(1)}, bf16[8,64,512]{2,1,0:T(8,128)(2,1)}, u32[]{:S(2)}) copy-start(bf16[8,64,512]{2,1,0:T(8,128)(2,1)} %copy-done.2) | copy-start | bytes 1572868 | tf_op jit(solution)/shard_map/while
  170.6 4.5 %copy-start.4 = (bf16[2,64,1,8,128]{4,3,1,0,2:T(8,128)(2,1)S(1)}, bf16[2,64,1,8,128]{4,3,1,0,2:T(8,128)(2,1)}, u32[]{:S(2)}) copy-start(bf16[2,64,1,8,128]{4,3,1,0,2:T(8,128)(2,1)} %get-tuple-element.294) | copy-start | bytes 786436 | tf_op jit(solution)/shard_map/while
  170.6 5.4 %copy-start.1 = (bf16[2048,1,128]{2,0,1:T(8,128)(2,1)S(1)}, bf16[2048,1,128]{2,0,1:T(8,128)(2,1)}, u32[]{:S(2)}) copy-start(bf16[2048,1,128]{2,0,1:T(8,128)(2,1)} %copy-done) | copy-start | bytes 1572868 | tf_op jit(solution)/shard_map/while
  175.3 0.7 copy-start.5
  176.0 7.2 %copy-start = (bf16[2048,1,128]{2,0,1:T(8,128)(2,1)}, bf16[2048,1,128]{2,0,1:T(8,128)(2,1)S(1)}, u32[]{:S(2)}) copy-start(bf16[2048,1,128]{2,0,1:T(8,128)(2,1)S(1)} %get-tuple-element.309) | copy-start | bytes 1572868 | tf_op jit(solution)/shard_map/while
  200.1 1.1 copy-start.2
  201.2 4.2 %copy-start.3 = (bf16[8,64,512]{2,1,0:T(8,128)(2,1)S(1)}, bf16[8,64,512]{2,1,0:T(8,128)(2,1)}, u32[]{:S(2)}) copy-start(bf16[8,64,512]{2,1,0:T(8,128)(2,1)} %copy-done.2) | copy-start | bytes 1572868 | tf_op jit(solution)/shard_map/while
  201.2 4.5 %copy-start.4 = (bf16[2,64,1,8,128]{4,3,1,0,2:T(8,128)(2,1)S(1)}, bf16[2,64,1,8,128]{4,3,1,0,2:T(8,128)(2,1)}, u32[]{:S(2)}) copy-start(bf16[2,64,1,8,128]{4,3,1,0,2:T(8,128)(2,1)} %get-tuple-element.294) | copy-start | bytes 786436 | tf_op jit(solution)/shard_map/while
  201.2 5.3 %copy-start.1 = (bf16[2048,1,128]{2,0,1:T(8,128)(2,1)S(1)}, bf16[2048,1,128]{2,0,1:T(8,128)(2,1)}, u32[]{:S(2)}) copy-start(bf16[2048,1,128]{2,0,1:T(8,128)(2,1)} %copy-done) | copy-start | bytes 1572868 | tf_op jit(solution)/shard_map/while
  205.9 0.7 copy-start.5
  206.7 1.1 copy-start.6
Sparse Core Ops, SparseCore 0:
  208.0 58.6 reduce-scatter.1
where the time goes:
time: 276 us; the launch traced here: 275 us
  other arithmetic  67.8 us (25%)
  waiting for transfers between devices  61.1 us (22%)
  local copies, waits for them, and re-layouts  56.7 us (21%)
  blocking collectives  38.3 us (14%)
  starting transfers between devices  25.2 us (9%)
  between operations  14.1 us (5%)
  matrix products  10.1 us (4%)
    reduce_scatter x1, waiting for transfers between devices, per_device(): lax.psum_scatter(jnp.concatenate([key_flat, value_flat], axis=1).astype(j...  58 us
    unnamed x1, other arithmetic  45.2 us
    all_gather x1, blocking collectives, per_device(): lax.all_gather(key_states, 'ctx', axis=1, tiled=True)  20.1 us
    all_gather x1, blocking collectives, per_device(): lax.all_gather(value_states, 'ctx', axis=1, tiled=True)  18.2 us
    ppermute x1, starting transfers between devices, shifted_2(): return lax.ppermute(value, axis, pairs)  17.9 us
    gather x2, local copies, waits for them, and re-layouts, block_step(): value_rows = value_table[row_index, head_index]  16.7 us
    unnamed x12, local copies, waits for them, and re-layouts  11.1 us
    scatter-add x2, other arithmetic, block_step(): key_sums = key_sums.at[row_index, head_index].add(key_part)  8.39 us
  transfers between devices with their start and end apart: 3, of which 2 were waited for; matrix products, arithmetic and copies ran while one was open for 1% of the time, Pallas kernels for 0%

commit v1 on v0

v1 whole, which is shorter than its diff:
```python
import functools

import jax
import jax.numpy as jnp
from jax import lax
from jax.experimental import pallas as pl
from jax.experimental.pallas import tpu as pltpu
from jax.sharding import PartitionSpec as P

HD = 128
BLK = 64
GROUP = 8
TILE_HEADS = 4
SCALE = HD ** (-0.5)
LOG2E = 1.4426950408889634
HIDDEN = -1e30

NT_DIMS = (((1,), (1,)), ((), ()))
TN_DIMS = (((0,), (0,)), ((), ()))


def rows_of(index, size):
    return pl.ds(pl.multiple_of(index * size, size), size)


def body(sizes, tbl, q, k, v, up, dq_out, dk_out, dv_out, *scratch):
    pipes, ctxs, heads, tok, topb = sizes
    (
        kbuf, vbuf, qv, og, qs, os, ks, pf, pb, dsb, part_v, part_k,
        av, ak, sbv, sbk, rbv, rbk, gv, gk, hv, hk,
        loc_sem, up_send, up_recv,
        k_send, k_recv, k_fwd, k_sib, v_send, v_recv, v_fwd, v_sib,
        ev_send, ev_recv, ek_send, ek_recv,
        rv_send, rv_recv, rk_send, rk_recv,
    ) = scratch
    chips = ctxs // 2
    blocks = tok // BLK
    all_blocks = ctxs * blocks
    slots = topb + 1
    tiles = GROUP // TILE_HEADS
    width = GROUP * HD
    keys = topb * BLK
    up_rows = tok // heads
    hidden_at = blocks * topb
    slot_at = 2 * blocks * topb

    z = lax.axis_index("pipe")
    c = lax.axis_index("ctx")
    y = lax.axis_index("head")
    x = c // 2
    core = c % 2
    other = c + 1 - 2 * core
    z_prev = (z + pipes - 1) % pipes
    z_next = (z + 1) % pipes

    def blocks_of(owner):
        return pl.ds(owner * blocks, blocks)

    def at_chip(chip):
        return (z, chip * 2 + core, y)

    sibling = (z, other, y)

    def remote(src, dst, send, recv, target):
        return pltpu.make_async_remote_copy(
            src_ref=src, dst_ref=dst, send_sem=send, recv_sem=recv,
            device_id=target, device_id_type=pl.DeviceIdType.MESH,
        )

    q_copy = pltpu.make_async_copy(q.at[0], qv, loc_sem.at[0])
    k_copy = pltpu.make_async_copy(k, kbuf.at[blocks_of(c)], loc_sem.at[1])
    v_copy = pltpu.make_async_copy(v, vbuf.at[blocks_of(c)], loc_sem.at[2])
    q_copy.start()
    k_copy.start()
    v_copy.start()

    barrier = pltpu.get_barrier_semaphore()

    def greet(target):
        pl.semaphore_signal(barrier, inc=1, device_id=target, device_id_type=pl.DeviceIdType.MESH)

    greet(sibling)

    def greet_chip(d, carry):
        greet(at_chip((x + d) % chips))
        return carry

    def greet_head(h, carry):
        greet((z_next, c, h))
        return carry

    lax.fori_loop(1, chips, greet_chip, 0)
    lax.fori_loop(0, heads, greet_head, 0)

    zero_rows = jnp.zeros((BLK, HD), jnp.float32)
    for qb in range(blocks):
        part_v[qb * slots + topb] = zero_rows
        part_k[qb * slots + topb] = zero_rows

    pl.semaphore_wait(barrier, heads + chips)

    def gather_copy(src, buf, send, recv, chip, target):
        return remote(src, buf.at[blocks_of(c)], send.at[chip], recv.at[x], target)

    def send_keys(chip, carry):
        gather_copy(k, kbuf, k_send, k_recv, chip, at_chip(chip)).start()
        return carry

    def send_values(chip, carry):
        gather_copy(v, vbuf, v_send, v_recv, chip, at_chip(chip)).start()
        return carry

    def up_copy(h):
        return remote(
            up.at[0, :, rows_of(h, width)], og.at[rows_of(y, up_rows)],
            up_send.at[h], up_recv.at[y], (z_prev, c, h),
        )

    def send_up(h, carry):
        up_copy(h).start()
        return carry

    lax.fori_loop(x + 1, chips, send_keys, 0)
    gather_copy(k, kbuf, k_send, k_sib, x, sibling).start()
    lax.fori_loop(0, heads, send_up, 0)
    lax.fori_loop(x + 1, chips, send_values, 0)
    gather_copy(v, vbuf, v_send, v_sib, x, sibling).start()

    def passed_on(buf, fwd, sib, chip):
        block = buf.at[blocks_of(chip * 2 + core)]
        return remote(block, block, fwd.at[chip], sib.at[chip], sibling)

    def arrived(buf, recv, chip):
        block = buf.at[blocks_of(chip * 2 + core)]
        return remote(block, block, recv.at[chip], recv.at[chip], sibling)

    def from_sibling(buf, sib, chip):
        block = buf.at[blocks_of(chip * 2 + 1 - core)]
        return remote(block, block, sib.at[chip], sib.at[chip], sibling)

    def forward_all(buf, recv, fwd, sib):
        def step(i, carry):
            chip = x - 1 - i
            arrived(buf, recv, chip).wait_recv()
            passed_on(buf, fwd, sib, chip).start()
            return carry

        lax.fori_loop(0, x, step, 0)

    def wait_sibling(buf, sib):
        def step(chip, carry):
            from_sibling(buf, sib, chip).wait_recv()
            return carry

        lax.fori_loop(0, x + 1, step, 0)

    forward_all(kbuf, k_recv, k_fwd, k_sib)
    q_copy.wait()
    k_copy.wait()
    v_copy.wait()
    wait_sibling(kbuf, k_sib)

    def chosen_rows(buf, qb):
        return jnp.concatenate([buf[tbl[qb * topb + t]] for t in range(topb)], axis=0)

    def head_rows(ref, qb, tile):
        return jnp.concatenate(
            [ref[rows_of(qb, BLK), rows_of(tile * TILE_HEADS + h, HD)] for h in range(TILE_HEADS)],
            axis=0,
        )

    columns = TILE_HEADS * BLK

    def score_step(i, carry):
        qb, tile = i // tiles, i % tiles
        key_rows = chosen_rows(kbuf, qb)
        ks[qb] = key_rows
        query_rows = head_rows(qv, qb, tile)
        qs[i] = query_rows
        scores = lax.dot_general(key_rows, query_rows, NT_DIMS, preferred_element_type=jnp.float32)
        key_at = lax.broadcasted_iota(jnp.int32, (BLK, columns), 0)
        query_at = lax.broadcasted_iota(jnp.int32, (BLK, columns), 1) % BLK
        pieces = [jnp.where(key_at <= query_at, scores[:BLK], -jnp.inf)]
        for t in range(1, topb):
            shift = tbl[hidden_at + qb * topb + t].astype(jnp.float32) * HIDDEN
            pieces.append(scores[t * BLK:(t + 1) * BLK] + shift)
        scores = jnp.concatenate(pieces, axis=0)
        top = jnp.max(scores, axis=0, keepdims=True)
        weights = jnp.exp2((scores - top) * (SCALE * LOG2E))
        weights = weights * (1.0 / jnp.sum(weights, axis=0, keepdims=True))
        pf[i] = weights
        pb[i] = weights.astype(jnp.bfloat16)
        return carry

    lax.fori_loop(0, blocks * tiles, score_step, 0)

    forward_all(vbuf, v_recv, v_fwd, v_sib)

    def up_arrived(h, carry):
        block = og.at[rows_of(h, up_rows)]
        remote(block, block, up_recv.at[h], up_recv.at[h], sibling).wait_recv()
        return carry

    lax.fori_loop(0, heads, up_arrived, 0)

    def block_sums(lhs, rhs, part):
        def step(qb, carry):
            total = jnp.dot(lhs[qb * tiles], rhs[qb * tiles], preferred_element_type=jnp.float32)
            for tile in range(1, tiles):
                total += jnp.dot(
                    lhs[qb * tiles + tile], rhs[qb * tiles + tile], preferred_element_type=jnp.float32
                )
            for t in range(topb):
                part[qb * slots + t] = total[t * BLK:(t + 1) * BLK]
            return carry

        lax.fori_loop(0, blocks, step, 0)

    def grad_rows(i, carry):
        os[i] = head_rows(og, i // tiles, i % tiles)
        return carry

    lax.fori_loop(0, blocks * tiles, grad_rows, 0)
    block_sums(pb, os, part_v)

    def exchange_copy(src, dst, send, recv, chip):
        return remote(
            src.at[rows_of(chip, tok)], dst.at[rows_of(chip, tok)], send.at[chip], recv.at[chip], sibling
        )

    def exchange(part, own, out, landing, send, recv):
        def owner_block(owner, b):
            j = owner * blocks + b
            total = part[tbl[slot_at + j]]
            for qb in range(1, blocks):
                total = total + part[tbl[slot_at + qb * all_blocks + j]]
            return total

        def step(chip, carry):
            for b in range(blocks):
                at = rows_of(chip * blocks + b, BLK)
                out[at, :] = owner_block(chip * 2 + 1 - core, b).astype(jnp.bfloat16)
            exchange_copy(out, landing, send, recv, chip).start()
            for b in range(blocks):
                at = rows_of(chip * blocks + b, BLK)
                own[at, :] = owner_block(chip * 2 + core, b)
            return carry

        lax.fori_loop(0, x + 1, step, 0)

    exchange(part_v, av, sbv, rbv, ev_send, ev_recv)

    wait_sibling(vbuf, v_sib)

    def score_grad_step(i, carry):
        qb = i // tiles
        value_rows = chosen_rows(vbuf, qb)
        weight_grad = lax.dot_general(value_rows, os[i], NT_DIMS, preferred_element_type=jnp.float32)
        weights = pf[i]
        delta = jnp.sum(weights * weight_grad, axis=0, keepdims=True)
        dsb[i] = (weights * (weight_grad - delta) * SCALE).astype(jnp.bfloat16)
        return carry

    lax.fori_loop(0, blocks * tiles, score_grad_step, 0)

    def owner_copy(src, dst, send, recv, chip):
        return remote(src.at[rows_of(chip, tok)], dst.at[x], send.at[chip], recv.at[x], at_chip(chip))

    def send_owned(own, src, landing, out, owners, send, landed, rsend, rrecv):
        def step(i, carry):
            chip = x - 1 - i
            at = rows_of(chip, tok)
            exchange_copy(src, landing, send, landed, chip).wait_recv()
            out[at, :] = (own[at, :] + landing[at, :].astype(jnp.float32)).astype(jnp.bfloat16)
            owner_copy(out, owners, rsend, rrecv, chip).start()
            return carry

        lax.fori_loop(0, x, step, 0)
        at = rows_of(x, tok)
        exchange_copy(src, landing, send, landed, x).wait_recv()
        own[at, :] = own[at, :] + landing[at, :].astype(jnp.float32)

    send_owned(av, sbv, rbv, gv, hv, ev_send, ev_recv, rv_send, rv_recv)

    block_sums(dsb, qs, part_k)
    exchange(part_k, ak, sbk, rbk, ek_send, ek_recv)

    def query_step(i, carry):
        qb, tile = i // tiles, i % tiles
        grad = lax.dot_general(dsb[i], ks[qb], TN_DIMS, preferred_element_type=jnp.float32)
        grad = grad.astype(jnp.bfloat16)
        for h in range(TILE_HEADS):
            dq_out[0, rows_of(qb, BLK), rows_of(tile * TILE_HEADS + h, HD)] = grad[h * BLK:(h + 1) * BLK]
        return carry

    lax.fori_loop(0, blocks * tiles, query_step, 0)
    send_owned(ak, sbk, rbk, gk, hk, ek_send, ek_recv, rk_send, rk_recv)

    def owned_total(own, landing, recv, out):
        own_rows = own[rows_of(x, tok), :]

        def step(chip, total):
            block = landing.at[chip]
            remote(block, block, recv.at[chip], recv.at[chip], sibling).wait_recv()
            return total + landing[chip].astype(jnp.float32)

        out[0] = lax.fori_loop(x + 1, chips, step, own_rows).astype(jnp.bfloat16)

    owned_total(av, hv, rv_recv, dv_out)
    owned_total(ak, hk, rk_recv, dk_out)

    def left_gather(chip, carry):
        gather_copy(k, kbuf, k_send, k_recv, chip, at_chip(chip)).wait_send()
        gather_copy(v, vbuf, v_send, v_recv, chip, at_chip(chip)).wait_send()
        return carry

    def left_up(h, carry):
        up_copy(h).wait_send()
        return carry

    def left_lower(chip, carry):
        passed_on(kbuf, k_fwd, k_sib, chip).wait_send()
        passed_on(vbuf, v_fwd, v_sib, chip).wait_send()
        owner_copy(gv, hv, rv_send, rv_recv, chip).wait_send()
        owner_copy(gk, hk, rk_send, rk_recv, chip).wait_send()
        return carry

    def left_exchange(chip, carry):
        exchange_copy(sbv, rbv, ev_send, ev_recv, chip).wait_send()
        exchange_copy(sbk, rbk, ek_send, ek_recv, chip).wait_send()
        return carry

    lax.fori_loop(x, chips, left_gather, 0)
    lax.fori_loop(0, heads, left_up, 0)
    lax.fori_loop(0, x, left_lower, 0)
    lax.fori_loop(0, x + 1, left_exchange, 0)


def block_table(selected, ctxs, blocks):
    chosen = selected[0, 0]
    topb = chosen.shape[1]
    mine = lax.axis_index("ctx") * blocks + jnp.arange(blocks, dtype=jnp.int32)[:, None]
    slot = jnp.arange(topb, dtype=jnp.int32)
    every = jnp.arange(ctxs * blocks, dtype=jnp.int32)
    found = chosen[:, :, None] == every
    slots = topb + jnp.sum(jnp.where(found, slot[:, None] - topb, 0), axis=1)
    slots = slots + (topb + 1) * jnp.arange(blocks, dtype=jnp.int32)[:, None]
    hidden = (chosen > mine).astype(jnp.int32)
    return jnp.concatenate(
        [jnp.minimum(chosen, mine).reshape(-1), hidden.reshape(-1), slots.reshape(-1)]
    )


def per_device(pipes, ctxs, heads, queries, key_states, value_states, upstream, selected):
    tok = queries.shape[1]
    topb = selected.shape[3]
    blocks = tok // BLK
    chips = ctxs // 2
    tokens = tok * ctxs
    keys = topb * BLK
    tiles = GROUP // TILE_HEADS
    columns = TILE_HEADS * BLK
    width = GROUP * HD
    bf16, f32 = jnp.bfloat16, jnp.float32
    vmem = pltpu.VMEM
    dma = pltpu.SemaphoreType.DMA
    owned = (chips * tok, HD)
    scratch = [
        vmem((tokens // BLK, BLK, HD), bf16), vmem((tokens // BLK, BLK, HD), bf16),
        vmem((tok, width), bf16), vmem((tok, width), bf16),
        vmem((blocks * tiles, columns, HD), bf16), vmem((blocks * tiles, columns, HD), bf16),
        vmem((blocks, keys, HD), bf16),
        vmem((blocks * tiles, keys, columns), f32), vmem((blocks * tiles, keys, columns), bf16),
        vmem((blocks * tiles, keys, columns), bf16),
        vmem((blocks * (topb + 1), BLK, HD), f32), vmem((blocks * (topb + 1), BLK, HD), f32),
        vmem(owned, f32), vmem(owned, f32),
        vmem(owned, bf16), vmem(owned, bf16), vmem(owned, bf16), vmem(owned, bf16),
        vmem(owned, bf16), vmem(owned, bf16),
        vmem((chips, tok, HD), bf16), vmem((chips, tok, HD), bf16),
        dma((3,)), dma((heads,)), dma((heads,)),
    ] + [dma((chips,)) for _ in range(16)]
    sizes = (pipes, ctxs, heads, tok, topb)
    whole = pl.BlockSpec(memory_space=pltpu.VMEM)
    hbm = pl.BlockSpec(memory_space=pl.ANY)
    return pl.pallas_call(
        functools.partial(body, sizes),
        out_shape=(
            jax.ShapeDtypeStruct(queries.shape, bf16),
            jax.ShapeDtypeStruct(key_states.shape, bf16),
            jax.ShapeDtypeStruct(value_states.shape, bf16),
        ),
        in_specs=[pl.BlockSpec(memory_space=pltpu.SMEM), hbm, hbm, hbm, hbm],
        out_specs=(whole, whole, whole),
        scratch_shapes=scratch,
        compiler_params=pltpu.CompilerParams(
            collective_id=0, has_side_effects=True, vmem_limit_bytes=48 * 1024 * 1024
        ),
        name="selected_attention_grads",
    )(
        block_table(selected, ctxs, blocks),
        queries,
        key_states.reshape(blocks, BLK, HD),
        value_states.reshape(blocks, BLK, HD),
        upstream,
    )


def solution(mesh):
    placed = (
        P("pipe", "ctx", "head"),
        P("pipe", "ctx", "head"),
        P("pipe", "ctx", "head"),
        P("pipe", ("ctx", "head"), None),
        P("pipe", "head", "ctx", None),
    )
    per = functools.partial(per_device, mesh.shape["pipe"], mesh.shape["ctx"], mesh.shape["head"])
    return jax.shard_map(
        per,
        mesh=mesh,
        in_specs=placed,
        out_specs=(P("pipe", "ctx", "head"), P("pipe", "ctx", "head"), P("pipe", "ctx", "head")),
        check_vma=False,
    )
```

time: 276 us -> 64.1 us (0.23)
  other arithmetic: 67.8 us -> 0.94 us
  waiting for transfers between devices: 61.1 us -> 0 us
  Pallas kernels: 0 us -> 56.4 us
  local copies, waits for them, and re-layouts: 56.7 us -> 5.6 us
  blocking collectives: 38.3 us -> 0 us
  starting transfers between devices: 25.2 us -> 0 us
  between operations: 14.1 us -> 0.67 us
  matrix products: 10.1 us -> 0 us
    reduce_scatter x1 -> x0, waiting for transfers between devices: 58 us -> none  [per_device(): lax.psum_scatter(jnp.concatenate([key_flat, value_flat], axis=1).astype(j...]
    pallas_call x0 -> x1, Pallas kernels: none -> 56.4 us  [per_device(): pl.pallas_call(functools.partial(body, sizes), out_shape=(jax.ShapeDtypeS...]
    unnamed x1 -> x0, other arithmetic: 45.2 us -> none
    all_gather x2 -> x0, blocking collectives: 38.3 us -> none  [the longest x1 20.1 us: per_device(): lax.all_gather(key_states, 'ctx', axis=1, tiled=True)]
    gather x4 -> x0, local copies, waits for them, and re-layouts: 21.7 us -> none  [the longest x2 16.7 us: block_step(): value_rows = value_table[row_index, head_index]]
    ppermute x1 -> x0, starting transfers between devices: 17.9 us -> none  [shifted_2(): return lax.ppermute(value, axis, pairs)]
    scatter-add x4 -> x0, other arithmetic: 16.5 us -> none  [the longest x2 8.39 us: block_step(): key_sums = key_sums.at[row_index, head_index].add(key_part)]
    dot_general x10 -> x0, matrix products: 10.1 us -> none  [the longest x2 2.63 us: block_step(): jnp.einsum('icgh,cjh->cgij', grad_blk, value_rows, preferred_element_type...]
  transfers between devices with their start and end apart: 3 -> 0, of which waited for: 2 -> 0; matrix products, arithmetic and copies ran while one was open for 1% -> 0% of each run, Pallas kernels for 0% -> 0%
where the time goes in v1:
time: 64.1 us; the launch traced here: 63.6 us
  Pallas kernels  56.4 us (88%)
  local copies, waits for them, and re-layouts  5.6 us (9%)
  other arithmetic  0.94 us (1%)
  between operations  0.67 us (1%)
    pallas_call x1, Pallas kernels, per_device(): pl.pallas_call(functools.partial(body, sizes), out_shape=(jax.ShapeDtypeS...  56.4 us
    unnamed x11, local copies, waits for them, and re-layouts  4.6 us

profile of v1, /device:TPU:1, one launch (start us, length us, event | category | flops | bytes accessed | tf_op | source)
XLA Modules:
  0.0 63.6 jit_solution(6918722354864734464)
XLA Ops:
  0.6 0.0 copy-start.2
  0.7 0.8 %squeeze.3 = s32[16]{0:T(128)S(1)} reshape(s32[1,1,2,8]{3,2,1,0:T(2,128)} %param.9) | data formatting | bytes 128 | tf_op jit(solution)/shard_map/squeeze | solution.py:340
  1.4 0.1 min.11
  1.5 0.1 min.12
  1.6 0.8 %select_reduce_fusion = s32[2,32]{1,0:T(2,128)S(1)} fusion(s32[8]{0:T(128)S(1)} %iota_add_fusion, s32[2,8]{1,0:T(2,128)} %bitcast.5), kind=kLoop, calls=%fused_computation | loop fusion | flops 1472 | bytes 352 | tf_op jit(solution)/shard_map/reduce_sum | solution.py:346
  2.4 0.1 add_add_fusion
  2.4 0.1 add.41
  2.5 0.1 pad_add_fusion.tbl
  2.6 0.0 copy-done.2
  2.6 0.0 copy-start
  2.6 0.9 %copy-done = bf16[1,128,1024]{2,1,0:T(8,128)(2,1)S(1)} copy-done((bf16[1,128,1024]{2,1,0:T(8,128)(2,1)S(1)}, bf16[1,128,1024]{2,1,0:T(8,128)(2,1)}, u32[]{:S(2)}) %copy-start) | copy-done | bytes 262168
  3.6 0.0 copy-start.1
  3.6 0.9 %copy-done.1 = bf16[1,16,8192]{2,1,0:T(8,128)(2,1)S(1)} copy-done((bf16[1,16,8192]{2,1,0:T(8,128)(2,1)S(1)}, bf16[1,16,8192]{2,1,0:T(8,128)(2,1)}, u32[]{:S(2)}) %copy-start.1) | copy-done | bytes 262168
  4.5 0.0 copy-start.3
  4.5 0.8 %copy-done.3 = bf16[1,128,128]{2,1,0:T(8,128)(2,1)S(1)} copy-done((bf16[1,128,128]{2,1,0:T(8,128)(2,1)S(1)}, bf16[1,128,128]{2,1,0:T(8,128)(2,1)}, u32[]{:S(2)}) %copy-start.3) | copy-done | bytes 32792
  5.3 56.4 %selected_attention_grads.1 = (bf16[1,128,1024]{2,1,0:T(8,128)(2,1)S(1)}, bf16[1,128,128]{2,1,0:T(8,128)(2,1)S(1)}, bf16[1,128,128]{2,1,0:T(8,128)(2,1)S(1)}) custom-call(s32[96]{0:T(128)S(1)} %pad_add_fusion.tbl, bf16[1,128,1024]{2,1,0:T(8,128)(2,1)S(1)} %copy-done, bf16[2,64,128]{2,1,0:T(8,128)(2,1)S(1)} %bitcast.3, bf16[2,64,128]{2,1,0:T(8,128)(2,1)S(1)} %bitcast.4, ...), custom_call_target="tpu_custom_call" | custom-call | tf_op jit(solution)/shard_map/selected_attention_grads/pallas_call | solution.py:385
  61.7 0.7 %copy.11 = bf16[1,128,1024]{2,1,0:T(8,128)(2,1)} copy(bf16[1,128,1024]{2,1,0:T(8,128)(2,1)S(1)} %get-tuple-element.6) | data formatting | bytes 524288
  62.4 0.6 copy.12
  63.0 0.6 copy.13
  (5 shorter events, 0.0 us)
Async XLA Ops:
  0.6 2.0 %copy-start.2 = (bf16[1,128,128]{2,1,0:T(8,128)(2,1)S(1)}, bf16[1,128,128]{2,1,0:T(8,128)(2,1)}, u32[]{:S(2)}) copy-start(bf16[1,128,128]{2,1,0:T(8,128)(2,1)} %param.6) | copy-start | bytes 98308
  2.6 1.0 %copy-start = (bf16[1,128,1024]{2,1,0:T(8,128)(2,1)S(1)}, bf16[1,128,1024]{2,1,0:T(8,128)(2,1)}, u32[]{:S(2)}) copy-start(bf16[1,128,1024]{2,1,0:T(8,128)(2,1)} %q.1) | copy-start | bytes 786436
  3.6 0.9 %copy-start.1 = (bf16[1,16,8192]{2,1,0:T(8,128)(2,1)S(1)}, bf16[1,16,8192]{2,1,0:T(8,128)(2,1)}, u32[]{:S(2)}) copy-start(bf16[1,16,8192]{2,1,0:T(8,128)(2,1)} %up.1) | copy-start | bytes 786436
  4.5 0.8 %copy-start.3 = (bf16[1,128,128]{2,1,0:T(8,128)(2,1)S(1)}, bf16[1,128,128]{2,1,0:T(8,128)(2,1)}, u32[]{:S(2)}) copy-start(bf16[1,128,128]{2,1,0:T(8,128)(2,1)} %param.7) | copy-start | bytes 98308

commit v2 on v1

--- a/solution.py
+++ b/solution.py
@@ -13,7 +13,6 @@
 TILE_HEADS = 4
 SCALE = HD ** (-0.5)
 LOG2E = 1.4426950408889634
-HIDDEN = -1e30
 
 NT_DIMS = (((1,), (1,)), ((), ()))
 TN_DIMS = (((0,), (0,)), ((), ()))
@@ -23,11 +22,11 @@
     return pl.ds(pl.multiple_of(index * size, size), size)
 
 
-def body(sizes, tbl, q, k, v, up, dq_out, dk_out, dv_out, *scratch):
+def body(sizes, sel_in, q, k, v, up, dq_out, dk_out, dv_out, *scratch):
     pipes, ctxs, heads, tok, topb = sizes
     (
         kbuf, vbuf, qv, og, qs, os, ks, pf, pb, dsb, part_v, part_k,
-        av, ak, sbv, sbk, rbv, rbk, gv, gk, hv, hk,
+        av, ak, sbv, sbk, rbv, rbk, gv, gk, hv, hk, sel, tbl, ready,
         loc_sem, up_send, up_recv,
         k_send, k_recv, k_fwd, k_sib, v_send, v_recv, v_fwd, v_sib,
         ev_send, ev_recv, ek_send, ek_recv,
@@ -41,8 +40,6 @@
     width = GROUP * HD
     keys = topb * BLK
     up_rows = tok // heads
-    hidden_at = blocks * topb
-    slot_at = 2 * blocks * topb
 
     z = lax.axis_index("pipe")
     c = lax.axis_index("ctx")
@@ -70,33 +67,33 @@
     q_copy = pltpu.make_async_copy(q.at[0], qv, loc_sem.at[0])
     k_copy = pltpu.make_async_copy(k, kbuf.at[blocks_of(c)], loc_sem.at[1])
     v_copy = pltpu.make_async_copy(v, vbuf.at[blocks_of(c)], loc_sem.at[2])
+    sel_copy = pltpu.make_async_copy(sel_in, sel, loc_sem.at[3])
+    sel_copy.start()
     q_copy.start()
     k_copy.start()
     v_copy.start()
 
     barrier = pltpu.get_barrier_semaphore()
 
-    def greet(target):
-        pl.semaphore_signal(barrier, inc=1, device_id=target, device_id_type=pl.DeviceIdType.MESH)
-
-    greet(sibling)
+    def greet(semaphore, target):
+        pl.semaphore_signal(semaphore, inc=1, device_id=target, device_id_type=pl.DeviceIdType.MESH)
+
+    greet(barrier, sibling)
 
     def greet_chip(d, carry):
-        greet(at_chip((x + d) % chips))
-        return carry
-
-    def greet_head(h, carry):
-        greet((z_next, c, h))
+        greet(barrier, at_chip((x + d) % chips))
+        return carry
+
+    def greet_receiver(h, carry):
+        greet(barrier, (z_prev, c, h))
+        return carry
+
+    def greet_sender(h, carry):
+        greet(ready, (z_next, c, h))
         return carry
 
     lax.fori_loop(1, chips, greet_chip, 0)
-    lax.fori_loop(0, heads, greet_head, 0)
-
-    zero_rows = jnp.zeros((BLK, HD), jnp.float32)
-    for qb in range(blocks):
-        part_v[qb * slots + topb] = zero_rows
-        part_k[qb * slots + topb] = zero_rows
-
+    lax.fori_loop(0, heads, greet_receiver, 0)
     pl.semaphore_wait(barrier, heads + chips)
 
     def gather_copy(src, buf, send, recv, chip, target):
@@ -122,9 +119,33 @@
 
     lax.fori_loop(x + 1, chips, send_keys, 0)
     gather_copy(k, kbuf, k_send, k_sib, x, sibling).start()
-    lax.fori_loop(0, heads, send_up, 0)
+    lax.fori_loop(0, heads, greet_sender, 0)
     lax.fori_loop(x + 1, chips, send_values, 0)
     gather_copy(v, vbuf, v_send, v_sib, x, sibling).start()
+
+    def send_all_up():
+        pl.semaphore_wait(ready, heads)
+        lax.fori_loop(0, heads, send_up, 0)
+
+    @pl.when(z > 0)
+    def _():
+        send_all_up()
+
+    sel_copy.wait()
+
+    def slot_row(j, carry):
+        for qb in range(blocks):
+            slot = jnp.int32(topb)
+            for t in range(topb):
+                slot = jnp.where(sel[0, 0, qb, t] == j, jnp.int32(t), slot)
+            tbl[qb * all_blocks + j] = slot + qb * slots
+        return carry
+
+    lax.fori_loop(0, all_blocks, slot_row, 0)
+    zero_rows = jnp.zeros((BLK, HD), jnp.float32)
+    for qb in range(blocks):
+        part_v[qb * slots + topb] = zero_rows
+        part_k[qb * slots + topb] = zero_rows
 
     def passed_on(buf, fwd, sib, chip):
         block = buf.at[blocks_of(chip * 2 + core)]
@@ -161,7 +182,10 @@
     wait_sibling(kbuf, k_sib)
 
     def chosen_rows(buf, qb):
-        return jnp.concatenate([buf[tbl[qb * topb + t]] for t in range(topb)], axis=0)
+        mine = c * blocks + qb
+        return jnp.concatenate(
+            [buf[jnp.minimum(sel[0, 0, qb, t], mine)] for t in range(topb)], axis=0
+        )
 
     def head_rows(ref, qb, tile):
         return jnp.concatenate(
@@ -173,6 +197,7 @@
 
     def score_step(i, carry):
         qb, tile = i // tiles, i % tiles
+        mine = c * blocks + qb
         key_rows = chosen_rows(kbuf, qb)
         ks[qb] = key_rows
         query_rows = head_rows(qv, qb, tile)
@@ -182,7 +207,7 @@
         query_at = lax.broadcasted_iota(jnp.int32, (BLK, columns), 1) % BLK
         pieces = [jnp.where(key_at <= query_at, scores[:BLK], -jnp.inf)]
         for t in range(1, topb):
-            shift = tbl[hidden_at + qb * topb + t].astype(jnp.float32) * HIDDEN
+            shift = jnp.where(sel[0, 0, qb, t] > mine, jnp.float32(-jnp.inf), jnp.float32(0.0))
             pieces.append(scores[t * BLK:(t + 1) * BLK] + shift)
         scores = jnp.concatenate(pieces, axis=0)
         top = jnp.max(scores, axis=0, keepdims=True)
@@ -193,6 +218,11 @@
         return carry
 
     lax.fori_loop(0, blocks * tiles, score_step, 0)
+
+    @pl.when(z == 0)
+    def _():
+        send_all_up()
+
 
     forward_all(vbuf, v_recv, v_fwd, v_sib)
 
@@ -231,9 +261,9 @@
     def exchange(part, own, out, landing, send, recv):
         def owner_block(owner, b):
             j = owner * blocks + b
-            total = part[tbl[slot_at + j]]
+            total = part[tbl[j]]
             for qb in range(1, blocks):
-                total = total + part[tbl[slot_at + qb * all_blocks + j]]
+                total = total + part[tbl[qb * all_blocks + j]]
             return total
 
         def step(chip, carry):
@@ -334,21 +364,6 @@
     lax.fori_loop(0, heads, left_up, 0)
     lax.fori_loop(0, x, left_lower, 0)
     lax.fori_loop(0, x + 1, left_exchange, 0)
-
-
-def block_table(selected, ctxs, blocks):
-    chosen = selected[0, 0]
-    topb = chosen.shape[1]
-    mine = lax.axis_index("ctx") * blocks + jnp.arange(blocks, dtype=jnp.int32)[:, None]
-    slot = jnp.arange(topb, dtype=jnp.int32)
-    every = jnp.arange(ctxs * blocks, dtype=jnp.int32)
-    found = chosen[:, :, None] == every
-    slots = topb + jnp.sum(jnp.where(found, slot[:, None] - topb, 0), axis=1)
-    slots = slots + (topb + 1) * jnp.arange(blocks, dtype=jnp.int32)[:, None]
-    hidden = (chosen > mine).astype(jnp.int32)
-    return jnp.concatenate(
-        [jnp.minimum(chosen, mine).reshape(-1), hidden.reshape(-1), slots.reshape(-1)]
-    )
 
 
 def per_device(pipes, ctxs, heads, queries, key_states, value_states, upstream, selected):
@@ -377,11 +392,14 @@
         vmem(owned, bf16), vmem(owned, bf16), vmem(owned, bf16), vmem(owned, bf16),
         vmem(owned, bf16), vmem(owned, bf16),
         vmem((chips, tok, HD), bf16), vmem((chips, tok, HD), bf16),
-        dma((3,)), dma((heads,)), dma((heads,)),
+        pltpu.SMEM((1, 1, blocks, topb), jnp.int32),
+        pltpu.SMEM((blocks * ctxs * blocks,), jnp.int32),
+        pltpu.SemaphoreType.REGULAR,
+        dma((4,)), dma((heads,)), dma((heads,)),
     ] + [dma((chips,)) for _ in range(16)]
     sizes = (pipes, ctxs, heads, tok, topb)
     whole = pl.BlockSpec(memory_space=pltpu.VMEM)
-    hbm = pl.BlockSpec(memory_space=pl.ANY)
+    hbm = pl.BlockSpec(memory_space=pltpu.HBM)
     return pl.pallas_call(
         functools.partial(body, sizes),
         out_shape=(
@@ -389,7 +407,7 @@
             jax.ShapeDtypeStruct(key_states.shape, bf16),
             jax.ShapeDtypeStruct(value_states.shape, bf16),
         ),
-        in_specs=[pl.BlockSpec(memory_space=pltpu.SMEM), hbm, hbm, hbm, hbm],
+        in_specs=[hbm] * 5,
         out_specs=(whole, whole, whole),
         scratch_shapes=scratch,
         compiler_params=pltpu.CompilerParams(
@@ -397,7 +415,7 @@
         ),
         name="selected_attention_grads",
     )(
-        block_table(selected, ctxs, blocks),
+        selected,
         queries,
         key_states.reshape(blocks, BLK, HD),
         value_states.reshape(blocks, BLK, HD),

time: 64.1 us -> 52.7 us (0.82)
  Pallas kernels: 56.4 us -> 45.7 us
  other arithmetic: 0.94 us -> 0 us
    pallas_call x1, Pallas kernels: 56.4 us -> 45.7 us  [per_device(): pl.pallas_call(functools.partial(body, sizes), out_shape=(jax.ShapeDtypeS...]
    unnamed x11 -> x13, local copies, waits for them, and re-layouts: 4.6 us -> 6.02 us
    reduce_sum x1 -> x0, other arithmetic: 0.77 us -> none  [block_table(): slots = topb + jnp.sum(jnp.where(found, slot[:, None] - topb, 0), axis=1)]
    squeeze x1 -> x0, local copies, waits for them, and re-layouts: 0.76 us -> none  [block_table(): chosen = selected[0, 0]]
where the time goes in v2:
time: 52.7 us; the launch traced here: 52.3 us
  Pallas kernels  45.7 us (87%)
  local copies, waits for them, and re-layouts  6.02 us (11%)
  between operations  0.65 us (1%)
    pallas_call x1, Pallas kernels, per_device(): pl.pallas_call(functools.partial(body, sizes), out_shape=(jax.ShapeDtypeS...  45.7 us
    unnamed x13, local copies, waits for them, and re-layouts  6.02 us

profile of v2, /device:TPU:1, one launch (start us, length us, event | category | flops | bytes accessed | tf_op | source)
XLA Modules:
  0.0 52.3 jit_solution(1630868434164011649)
XLA Ops:
  0.6 0.0 copy-start.4
  0.6 0.7 %copy-done.4 = s32[1,1,2,8]{3,2,1,0:T(2,128)S(1)} copy-done((s32[1,1,2,8]{3,2,1,0:T(2,128)S(1)}, s32[1,1,2,8]{3,2,1,0:T(2,128)}, u32[]{:S(2)}) %copy-start.4) | copy-done | bytes 88
  1.3 0.0 copy-start
  1.3 0.9 %copy-done = bf16[1,128,1024]{2,1,0:T(8,128)(2,1)S(1)} copy-done((bf16[1,128,1024]{2,1,0:T(8,128)(2,1)S(1)}, bf16[1,128,1024]{2,1,0:T(8,128)(2,1)}, u32[]{:S(2)}) %copy-start) | copy-done | bytes 262168
  2.3 0.0 copy-start.1
  2.3 0.9 %copy-done.1 = bf16[1,16,8192]{2,1,0:T(8,128)(2,1)S(1)} copy-done((bf16[1,16,8192]{2,1,0:T(8,128)(2,1)S(1)}, bf16[1,16,8192]{2,1,0:T(8,128)(2,1)}, u32[]{:S(2)}) %copy-start.1) | copy-done | bytes 262168
  3.2 0.0 copy-start.2
  3.2 0.8 %copy-done.2 = bf16[1,128,128]{2,1,0:T(8,128)(2,1)S(1)} copy-done((bf16[1,128,128]{2,1,0:T(8,128)(2,1)S(1)}, bf16[1,128,128]{2,1,0:T(8,128)(2,1)}, u32[]{:S(2)}) %copy-start.2) | copy-done | bytes 32792
  4.0 0.0 copy-start.3
  4.0 0.8 %copy-done.3 = bf16[1,128,128]{2,1,0:T(8,128)(2,1)S(1)} copy-done((bf16[1,128,128]{2,1,0:T(8,128)(2,1)S(1)}, bf16[1,128,128]{2,1,0:T(8,128)(2,1)}, u32[]{:S(2)}) %copy-start.3) | copy-done | bytes 32792
  4.7 45.7 %selected_attention_grads.1 = (bf16[1,128,1024]{2,1,0:T(8,128)(2,1)S(1)}, bf16[1,128,128]{2,1,0:T(8,128)(2,1)S(1)}, bf16[1,128,128]{2,1,0:T(8,128)(2,1)S(1)}) custom-call(s32[1,1,2,8]{3,2,1,0:T(2,128)S(1)} %copy-done.4, bf16[1,128,1024]{2,1,0:T(8,128)(2,1)S(1)} %copy-done, bf16[2,64,128]{2,1,0:T(8,128)(2,1)S(1)} %bitcast.2, bf16[2,64,128]{2,1,0:T(8,128)(2,1)S(1)} %bitcast.3, ...), custom_call_target="tpu_custom_call" | custom-call | tf_op jit(solution)/shard_map/selected_attention_grads/pallas_call | solution.py:403
  50.4 0.7 %copy.11 = bf16[1,128,1024]{2,1,0:T(8,128)(2,1)} copy(bf16[1,128,1024]{2,1,0:T(8,128)(2,1)S(1)} %get-tuple-element.6) | data formatting | bytes 524288
  51.1 0.6 %copy.12 = bf16[1,128,128]{2,1,0:T(8,128)(2,1)} copy(bf16[1,128,128]{2,1,0:T(8,128)(2,1)S(1)} %get-tuple-element.7) | data formatting | bytes 65536
  51.7 0.6 %copy.13 = bf16[1,128,128]{2,1,0:T(8,128)(2,1)} copy(bf16[1,128,128]{2,1,0:T(8,128)(2,1)S(1)} %get-tuple-element.8) | data formatting | bytes 65536
Async XLA Ops:
  0.6 0.7 %copy-start.4 = (s32[1,1,2,8]{3,2,1,0:T(2,128)S(1)}, s32[1,1,2,8]{3,2,1,0:T(2,128)}, u32[]{:S(2)}) copy-start(s32[1,1,2,8]{3,2,1,0:T(2,128)} %sel_in.1) | copy-start | bytes 196
  1.3 0.9 %copy-start = (bf16[1,128,1024]{2,1,0:T(8,128)(2,1)S(1)}, bf16[1,128,1024]{2,1,0:T(8,128)(2,1)}, u32[]{:S(2)}) copy-start(bf16[1,128,1024]{2,1,0:T(8,128)(2,1)} %q.1) | copy-start | bytes 786436
  2.3 0.9 %copy-start.1 = (bf16[1,16,8192]{2,1,0:T(8,128)(2,1)S(1)}, bf16[1,16,8192]{2,1,0:T(8,128)(2,1)}, u32[]{:S(2)}) copy-start(bf16[1,16,8192]{2,1,0:T(8,128)(2,1)} %up.1) | copy-start | bytes 786436
  3.2 0.8 %copy-start.2 = (bf16[1,128,128]{2,1,0:T(8,128)(2,1)S(1)}, bf16[1,128,128]{2,1,0:T(8,128)(2,1)}, u32[]{:S(2)}) copy-start(bf16[1,128,128]{2,1,0:T(8,128)(2,1)} %param.6) | copy-start | bytes 98308
  4.0 0.8 %copy-start.3 = (bf16[1,128,128]{2,1,0:T(8,128)(2,1)S(1)}, bf16[1,128,128]{2,1,0:T(8,128)(2,1)}, u32[]{:S(2)}) copy-start(bf16[1,128,128]{2,1,0:T(8,128)(2,1)} %param.7) | copy-start | bytes 98308

commit v3 on v2

--- a/solution.py
+++ b/solution.py
@@ -26,7 +26,7 @@
     pipes, ctxs, heads, tok, topb = sizes
     (
         kbuf, vbuf, qv, og, qs, os, ks, pf, pb, dsb, part_v, part_k,
-        av, ak, sbv, sbk, rbv, rbk, gv, gk, hv, hk, sel, tbl, ready,
+        av, ak, sbv, sbk, rbv, rbk, gv, gk, hv, hk, dq, dkv, sel, tbl, ready,
         loc_sem, up_send, up_recv,
         k_send, k_recv, k_fwd, k_sib, v_send, v_recv, v_fwd, v_sib,
         ev_send, ev_recv, ek_send, ek_recv,
@@ -75,13 +75,20 @@
 
     barrier = pltpu.get_barrier_semaphore()
 
+    def told_later(section):
+        return jnp.logical_or(section == 0, jnp.logical_and(section == 1, c == 0))
+
+    def as_int(flag):
+        return jnp.where(flag, jnp.int32(1), jnp.int32(0))
+
+    late = told_later(z)
+    next_late = told_later(z_next)
+
     def greet(semaphore, target):
         pl.semaphore_signal(semaphore, inc=1, device_id=target, device_id_type=pl.DeviceIdType.MESH)
 
-    greet(barrier, sibling)
-
-    def greet_chip(d, carry):
-        greet(barrier, at_chip((x + d) % chips))
+    def greet_chip(chip, carry):
+        greet(barrier, at_chip(chip))
         return carry
 
     def greet_receiver(h, carry):
@@ -89,12 +96,32 @@
         return carry
 
     def greet_sender(h, carry):
+        greet(barrier, (z_next, c, h))
+        return carry
+
+    def tell_sender(h, carry):
         greet(ready, (z_next, c, h))
         return carry
 
-    lax.fori_loop(1, chips, greet_chip, 0)
-    lax.fori_loop(0, heads, greet_receiver, 0)
-    pl.semaphore_wait(barrier, heads + chips)
+    lax.fori_loop(0, x, greet_chip, 0)
+
+    @pl.when(core == 1)
+    def _():
+        greet(barrier, sibling)
+
+    @pl.when(jnp.logical_not(next_late))
+    def _():
+        lax.fori_loop(0, heads, greet_sender, 0)
+
+    @pl.when(late)
+    def _():
+        lax.fori_loop(0, heads, greet_receiver, 0)
+
+    expected = chips - 1 - x + (1 - core) + heads * (1 - as_int(late)) + heads * as_int(next_late)
+
+    @pl.when(expected > 0)
+    def _():
+        pl.semaphore_wait(barrier, expected)
 
     def gather_copy(src, buf, send, recv, chip, target):
         return remote(src, buf.at[blocks_of(c)], send.at[chip], recv.at[x], target)
@@ -106,6 +133,10 @@
     def send_values(chip, carry):
         gather_copy(v, vbuf, v_send, v_recv, chip, at_chip(chip)).start()
         return carry
+
+    def send_to_sibling():
+        gather_copy(k, kbuf, k_send, k_sib, x, sibling).start()
+        gather_copy(v, vbuf, v_send, v_sib, x, sibling).start()
 
     def up_copy(h):
         return remote(
@@ -118,18 +149,20 @@
         return carry
 
     lax.fori_loop(x + 1, chips, send_keys, 0)
-    gather_copy(k, kbuf, k_send, k_sib, x, sibling).start()
-    lax.fori_loop(0, heads, greet_sender, 0)
+
+    @pl.when(core == 0)
+    def _():
+        send_to_sibling()
+
     lax.fori_loop(x + 1, chips, send_values, 0)
-    gather_copy(v, vbuf, v_send, v_sib, x, sibling).start()
-
-    def send_all_up():
-        pl.semaphore_wait(ready, heads)
+
+    @pl.when(next_late)
+    def _():
+        lax.fori_loop(0, heads, tell_sender, 0)
+
+    @pl.when(jnp.logical_not(late))
+    def _():
         lax.fori_loop(0, heads, send_up, 0)
-
-    @pl.when(z > 0)
-    def _():
-        send_all_up()
 
     sel_copy.wait()
 
@@ -168,18 +201,23 @@
 
         lax.fori_loop(0, x, step, 0)
 
-    def wait_sibling(buf, sib):
+    def wait_sibling(buf, sib, count):
         def step(chip, carry):
             from_sibling(buf, sib, chip).wait_recv()
             return carry
 
-        lax.fori_loop(0, x + 1, step, 0)
+        lax.fori_loop(0, count, step, 0)
+
+    @pl.when(core == 1)
+    def _():
+        from_sibling(kbuf, k_sib, x).wait_recv()
+        send_to_sibling()
 
     forward_all(kbuf, k_recv, k_fwd, k_sib)
     q_copy.wait()
     k_copy.wait()
     v_copy.wait()
-    wait_sibling(kbuf, k_sib)
+    wait_sibling(kbuf, k_sib, x + 1 - core)
 
     def chosen_rows(buf, qb):
         mine = c * blocks + qb
@@ -219,11 +257,6 @@
 
     lax.fori_loop(0, blocks * tiles, score_step, 0)
 
-    @pl.when(z == 0)
-    def _():
-        send_all_up()
-
-
     forward_all(vbuf, v_recv, v_fwd, v_sib)
 
     def up_arrived(h, carry):
@@ -280,7 +313,7 @@
 
     exchange(part_v, av, sbv, rbv, ev_send, ev_recv)
 
-    wait_sibling(vbuf, v_sib)
+    wait_sibling(vbuf, v_sib, x + 1)
 
     def score_grad_step(i, carry):
         qb = i // tiles
@@ -312,6 +345,12 @@
 
     send_owned(av, sbv, rbv, gv, hv, ev_send, ev_recv, rv_send, rv_recv)
 
+    @pl.when(late)
+    def _():
+        pl.semaphore_wait(ready, heads)
+        lax.fori_loop(0, heads, send_up, 0)
+
+
     block_sums(dsb, qs, part_k)
     exchange(part_k, ak, sbk, rbk, ek_send, ek_recv)
 
@@ -320,13 +359,15 @@
         grad = lax.dot_general(dsb[i], ks[qb], TN_DIMS, preferred_element_type=jnp.float32)
         grad = grad.astype(jnp.bfloat16)
         for h in range(TILE_HEADS):
-            dq_out[0, rows_of(qb, BLK), rows_of(tile * TILE_HEADS + h, HD)] = grad[h * BLK:(h + 1) * BLK]
+            dq[rows_of(qb, BLK), rows_of(tile * TILE_HEADS + h, HD)] = grad[h * BLK:(h + 1) * BLK]
         return carry
 
     lax.fori_loop(0, blocks * tiles, query_step, 0)
+    dq_copy = pltpu.make_async_copy(dq, dq_out.at[0], loc_sem.at[4])
+    dq_copy.start()
     send_owned(ak, sbk, rbk, gk, hk, ek_send, ek_recv, rk_send, rk_recv)
 
-    def owned_total(own, landing, recv, out):
+    def owned_total(own, landing, recv, at):
         own_rows = own[rows_of(x, tok), :]
 
         def step(chip, total):
@@ -334,10 +375,14 @@
             remote(block, block, recv.at[chip], recv.at[chip], sibling).wait_recv()
             return total + landing[chip].astype(jnp.float32)
 
-        out[0] = lax.fori_loop(x + 1, chips, step, own_rows).astype(jnp.bfloat16)
-
-    owned_total(av, hv, rv_recv, dv_out)
-    owned_total(ak, hk, rk_recv, dk_out)
+        dkv[at] = lax.fori_loop(x + 1, chips, step, own_rows).astype(jnp.bfloat16)
+
+    owned_total(av, hv, rv_recv, 0)
+    dv_copy = pltpu.make_async_copy(dkv.at[0], dv_out.at[0], loc_sem.at[5])
+    dv_copy.start()
+    owned_total(ak, hk, rk_recv, 1)
+    dk_copy = pltpu.make_async_copy(dkv.at[1], dk_out.at[0], loc_sem.at[6])
+    dk_copy.start()
 
     def left_gather(chip, carry):
         gather_copy(k, kbuf, k_send, k_recv, chip, at_chip(chip)).wait_send()
@@ -364,6 +409,18 @@
     lax.fori_loop(0, heads, left_up, 0)
     lax.fori_loop(0, x, left_lower, 0)
     lax.fori_loop(0, x + 1, left_exchange, 0)
+    dq_copy.wait()
+    dv_copy.wait()
+    dk_copy.wait()
+
+
+def hand_on(dq_in, dk_in, dv_in, dq_out, dk_out, dv_out, sems):
+    pairs = ((dq_in, dq_out), (dk_in, dk_out), (dv_in, dv_out))
+    copies = [pltpu.make_async_copy(a, b, sems.at[i]) for i, (a, b) in enumerate(pairs)]
+    for copy in copies:
+        copy.start()
+    for copy in copies:
+        copy.wait()
 
 
 def per_device(pipes, ctxs, heads, queries, key_states, value_states, upstream, selected):
@@ -392,26 +449,27 @@
         vmem(owned, bf16), vmem(owned, bf16), vmem(owned, bf16), vmem(owned, bf16),
         vmem(owned, bf16), vmem(owned, bf16),
         vmem((chips, tok, HD), bf16), vmem((chips, tok, HD), bf16),
+        vmem((tok, width), bf16), vmem((2, tok, HD), bf16),
         pltpu.SMEM((1, 1, blocks, topb), jnp.int32),
         pltpu.SMEM((blocks * ctxs * blocks,), jnp.int32),
         pltpu.SemaphoreType.REGULAR,
-        dma((4,)), dma((heads,)), dma((heads,)),
+        dma((7,)), dma((heads,)), dma((heads,)),
     ] + [dma((chips,)) for _ in range(16)]
     sizes = (pipes, ctxs, heads, tok, topb)
-    whole = pl.BlockSpec(memory_space=pltpu.VMEM)
     hbm = pl.BlockSpec(memory_space=pltpu.HBM)
-    return pl.pallas_call(
+    results = (
+        jax.ShapeDtypeStruct(queries.shape, bf16),
+        jax.ShapeDtypeStruct(key_states.shape, bf16),
+        jax.ShapeDtypeStruct(value_states.shape, bf16),
+    )
+    grads = pl.pallas_call(
         functools.partial(body, sizes),
-        out_shape=(
-            jax.ShapeDtypeStruct(queries.shape, bf16),
-            jax.ShapeDtypeStruct(key_states.shape, bf16),
-            jax.ShapeDtypeStruct(value_states.shape, bf16),
-        ),
+        out_shape=results,
         in_specs=[hbm] * 5,
-        out_specs=(whole, whole, whole),
+        out_specs=(hbm, hbm, hbm),
         scratch_shapes=scratch,
         compiler_params=pltpu.CompilerParams(
-            collective_id=0, has_side_effects=True, vmem_limit_bytes=48 * 1024 * 1024
+            collective_id=0, has_side_effects=True, vmem_limit_bytes=60 * 1024 * 1024
         ),
         name="selected_attention_grads",
     )(
@@ -421,6 +479,15 @@
         value_states.reshape(blocks, BLK, HD),
         upstream,
     )
+    return pl.pallas_call(
+        hand_on,
+        out_shape=results,
+        in_specs=[hbm] * 3,
+        out_specs=(hbm, hbm, hbm),
+        scratch_shapes=[dma((3,))],
+        compiler_params=pltpu.CompilerParams(vmem_limit_bytes=60 * 1024 * 1024),
+        name="hand_on_grads",
+    )(*grads)
 
 
 def solution(mesh):

time: 52.7 us -> 58.2 us (1.10)
  the two profiles are of different devices: /device:TPU:1 before, /device:TPU:658 now
where the time goes in v3:
time: 58.2 us; the launch traced here: 58 us
  Pallas kernels  57.4 us (99%)
  between operations  0.64 us (1%)
    pallas_call x1, Pallas kernels, per_device(): pl.pallas_call(functools.partial(body, sizes), out_shape=results, in_spec...  46.3 us
    pallas_call x1, Pallas kernels, per_device(): pl.pallas_call(hand_on, out_shape=results, in_specs=[hbm] * 3, out_specs=...  11.1 us

profile of v3, /device:TPU:658, one launch (start us, length us, event | category | flops | bytes accessed | tf_op | source)
XLA Modules:
  0.0 58.0 jit_solution(17086071104782558110)
XLA Ops:
  0.6 46.3 %selected_attention_grads.1 = (bf16[1,128,1024]{2,1,0:T(8,128)(2,1)}, bf16[1,128,128]{2,1,0:T(8,128)(2,1)}, bf16[1,128,128]{2,1,0:T(8,128)(2,1)}) custom-call(s32[1,1,2,8]{3,2,1,0:T(2,128)} %sel_in.1, bf16[1,128,1024]{2,1,0:T(8,128)(2,1)} %q.1, bf16[2,64,128]{2,1,0:T(8,128)(2,1)} %bitcast.2, bf16[2,64,128]{2,1,0:T(8,128)(2,1)} %bitcast.3, ...), custom_call_target="tpu_custom_call" | custom-call | tf_op jit(solution)/shard_map/selected_attention_grads/pallas_call | solution.py:465
  47.0 11.1 %hand_on_grads.1 = (bf16[1,128,1024]{2,1,0:T(8,128)(2,1)}, bf16[1,128,128]{2,1,0:T(8,128)(2,1)}, bf16[1,128,128]{2,1,0:T(8,128)(2,1)}) custom-call(bf16[1,128,1024]{2,1,0:T(8,128)(2,1)} %get-tuple-element.6.dq_in, bf16[1,128,128]{2,1,0:T(8,128)(2,1)} %get-tuple-element.7.dk_in, bf16[1,128,128]{2,1,0:T(8,128)(2,1)} %get-tuple-element.8.dv_in), custom_call_target="tpu_custom_call" | custom-call | tf_op jit(solution)/shard_map/hand_on_grads/pallas_call | solution.py:482

commit v4 on v3

--- a/solution.py
+++ b/solution.py
@@ -57,6 +57,20 @@
         return (z, chip * 2 + core, y)
 
     sibling = (z, other, y)
+    near_first = sorted(range(1, chips), key=lambda d: min(d, chips - d))
+
+    def later_chips(step):
+        for d in reversed(near_first):
+            @pl.when(x + d < chips)
+            def _(d=d):
+                step(x + d)
+
+    def earlier_chips(step, order):
+        for d in order:
+            @pl.when(x >= d)
+            def _(d=d):
+                step(x - d)
+
 
     def remote(src, dst, send, recv, target):
         return pltpu.make_async_remote_copy(
@@ -126,13 +140,11 @@
     def gather_copy(src, buf, send, recv, chip, target):
         return remote(src, buf.at[blocks_of(c)], send.at[chip], recv.at[x], target)
 
-    def send_keys(chip, carry):
+    def send_keys(chip):
         gather_copy(k, kbuf, k_send, k_recv, chip, at_chip(chip)).start()
-        return carry
-
-    def send_values(chip, carry):
+
+    def send_values(chip):
         gather_copy(v, vbuf, v_send, v_recv, chip, at_chip(chip)).start()
-        return carry
 
     def send_to_sibling():
         gather_copy(k, kbuf, k_send, k_sib, x, sibling).start()
@@ -148,13 +160,11 @@
         up_copy(h).start()
         return carry
 
-    lax.fori_loop(x + 1, chips, send_keys, 0)
+    later_chips(send_keys)
 
     @pl.when(core == 0)
     def _():
         send_to_sibling()
-
-    lax.fori_loop(x + 1, chips, send_values, 0)
 
     @pl.when(next_late)
     def _():
@@ -193,13 +203,11 @@
         return remote(block, block, sib.at[chip], sib.at[chip], sibling)
 
     def forward_all(buf, recv, fwd, sib):
-        def step(i, carry):
-            chip = x - 1 - i
+        def step(chip):
             arrived(buf, recv, chip).wait_recv()
             passed_on(buf, fwd, sib, chip).start()
-            return carry
-
-        lax.fori_loop(0, x, step, 0)
+
+        earlier_chips(step, near_first)
 
     def wait_sibling(buf, sib, count):
         def step(chip, carry):
@@ -207,6 +215,13 @@
             return carry
 
         lax.fori_loop(0, count, step, 0)
+
+    def keys_left(chip, carry):
+        gather_copy(k, kbuf, k_send, k_recv, chip, at_chip(chip)).wait_send()
+        return carry
+
+    lax.fori_loop(x + 1, chips, keys_left, 0)
+    later_chips(send_values)
 
     @pl.when(core == 1)
     def _():
@@ -257,8 +272,6 @@
 
     lax.fori_loop(0, blocks * tiles, score_step, 0)
 
-    forward_all(vbuf, v_recv, v_fwd, v_sib)
-
     def up_arrived(h, carry):
         block = og.at[rows_of(h, up_rows)]
         remote(block, block, up_recv.at[h], up_recv.at[h], sibling).wait_recv()
@@ -313,8 +326,6 @@
 
     exchange(part_v, av, sbv, rbv, ev_send, ev_recv)
 
-    wait_sibling(vbuf, v_sib, x + 1)
-
     def score_grad_step(i, carry):
         qb = i // tiles
         value_rows = chosen_rows(vbuf, qb)
@@ -324,26 +335,24 @@
         dsb[i] = (weights * (weight_grad - delta) * SCALE).astype(jnp.bfloat16)
         return carry
 
-    lax.fori_loop(0, blocks * tiles, score_grad_step, 0)
 
     def owner_copy(src, dst, send, recv, chip):
         return remote(src.at[rows_of(chip, tok)], dst.at[x], send.at[chip], recv.at[x], at_chip(chip))
 
     def send_owned(own, src, landing, out, owners, send, landed, rsend, rrecv):
-        def step(i, carry):
-            chip = x - 1 - i
+        def step(chip):
             at = rows_of(chip, tok)
             exchange_copy(src, landing, send, landed, chip).wait_recv()
             out[at, :] = (own[at, :] + landing[at, :].astype(jnp.float32)).astype(jnp.bfloat16)
             owner_copy(out, owners, rsend, rrecv, chip).start()
-            return carry
-
-        lax.fori_loop(0, x, step, 0)
+
+        earlier_chips(step, near_first[::-1])
         at = rows_of(x, tok)
         exchange_copy(src, landing, send, landed, x).wait_recv()
         own[at, :] = own[at, :] + landing[at, :].astype(jnp.float32)
 
     send_owned(av, sbv, rbv, gv, hv, ev_send, ev_recv, rv_send, rv_recv)
+    forward_all(vbuf, v_recv, v_fwd, v_sib)
 
     @pl.when(late)
     def _():
@@ -351,6 +360,8 @@
         lax.fori_loop(0, heads, send_up, 0)
 
 
+    wait_sibling(vbuf, v_sib, x + 1)
+    lax.fori_loop(0, blocks * tiles, score_grad_step, 0)
     block_sums(dsb, qs, part_k)
     exchange(part_k, ak, sbk, rbk, ek_send, ek_recv)
 
@@ -385,7 +396,10 @@
     dk_copy.start()
 
     def left_gather(chip, carry):
-        gather_copy(k, kbuf, k_send, k_recv, chip, at_chip(chip)).wait_send()
+        @pl.when(chip == x)
+        def _():
+            gather_copy(k, kbuf, k_send, k_recv, chip, at_chip(chip)).wait_send()
+
         gather_copy(v, vbuf, v_send, v_recv, chip, at_chip(chip)).wait_send()
         return carry
 
@@ -414,13 +428,10 @@
     dk_copy.wait()
 
 
-def hand_on(dq_in, dk_in, dv_in, dq_out, dk_out, dv_out, sems):
-    pairs = ((dq_in, dq_out), (dk_in, dk_out), (dv_in, dv_out))
-    copies = [pltpu.make_async_copy(a, b, sems.at[i]) for i, (a, b) in enumerate(pairs)]
-    for copy in copies:
-        copy.start()
-    for copy in copies:
-        copy.wait()
+def hand_on(dq_in, dk_in, dv_in, dq_out, dk_out, dv_out):
+    dq_out[...] = dq_in[...]
+    dk_out[...] = dk_in[...]
+    dv_out[...] = dv_in[...]
 
 
 def per_device(pipes, ctxs, heads, queries, key_states, value_states, upstream, selected):
@@ -479,13 +490,12 @@
         value_states.reshape(blocks, BLK, HD),
         upstream,
     )
+    whole = pl.BlockSpec(memory_space=pltpu.VMEM)
     return pl.pallas_call(
         hand_on,
         out_shape=results,
-        in_specs=[hbm] * 3,
-        out_specs=(hbm, hbm, hbm),
-        scratch_shapes=[dma((3,))],
-        compiler_params=pltpu.CompilerParams(vmem_limit_bytes=60 * 1024 * 1024),
+        in_specs=[whole] * 3,
+        out_specs=(whole, whole, whole),
         name="hand_on_grads",
     )(*grads)
 

time: 58.2 us -> 43.9 us (0.75)
  the two profiles are of different devices: /device:TPU:658 before, /device:TPU:1 now
where the time goes in v4:
time: 43.9 us; the launch traced here: 43.8 us
  Pallas kernels  43.1 us (98%)
  between operations  0.64 us (1%)
    pallas_call x1, Pallas kernels, per_device(): pl.pallas_call(functools.partial(body, sizes), out_shape=results, in_spec...  41.4 us
    pallas_call x1, Pallas kernels, per_device(): pl.pallas_call(hand_on, out_shape=results, in_specs=[whole] * 3, out_spec...  1.7 us

profile of v4, /device:TPU:1, one launch (start us, length us, event | category | flops | bytes accessed | tf_op | source)
XLA Modules:
  0.0 43.8 jit_solution(12029514569420536301)
XLA Ops:
  0.6 41.4 %selected_attention_grads.1 = (bf16[1,128,1024]{2,1,0:T(8,128)(2,1)}, bf16[1,128,128]{2,1,0:T(8,128)(2,1)}, bf16[1,128,128]{2,1,0:T(8,128)(2,1)}) custom-call(s32[1,1,2,8]{3,2,1,0:T(2,128)} %sel_in.1, bf16[1,128,1024]{2,1,0:T(8,128)(2,1)} %q.1, bf16[2,64,128]{2,1,0:T(8,128)(2,1)} %bitcast.2, bf16[2,64,128]{2,1,0:T(8,128)(2,1)} %bitcast.3, ...), custom_call_target="tpu_custom_call" | custom-call | tf_op jit(solution)/shard_map/selected_attention_grads/pallas_call | solution.py:476
  42.1 1.7 %hand_on_grads.1 = (bf16[1,128,1024]{2,1,0:T(8,128)(2,1)}, bf16[1,128,128]{2,1,0:T(8,128)(2,1)}, bf16[1,128,128]{2,1,0:T(8,128)(2,1)}) custom-call(bf16[1,128,1024]{2,1,0:T(8,128)(2,1)} %get-tuple-element.6.dq_in, bf16[1,128,128]{2,1,0:T(8,128)(2,1)} %get-tuple-element.7.dk_in, bf16[1,128,128]{2,1,0:T(8,128)(2,1)} %get-tuple-element.8.dv_in), custom_call_target="tpu_custom_call" | custom-call | tf_op jit(solution)/shard_map/hand_on_grads/pallas_call | solution.py:494

commit v5 on v4

--- a/solution.py
+++ b/solution.py
@@ -67,9 +67,13 @@
 
     def earlier_chips(step, order):
         for d in order:
-            @pl.when(x >= d)
+            @pl.when(x > d)
             def _(d=d):
                 step(x - d)
+
+        @pl.when(x > 0)
+        def _():
+            step(0)
 
 
     def remote(src, dst, send, recv, target):
@@ -153,7 +157,7 @@
     def up_copy(h):
         return remote(
             up.at[0, :, rows_of(h, width)], og.at[rows_of(y, up_rows)],
-            up_send.at[h], up_recv.at[y], (z_prev, c, h),
+            up_send, up_recv, (z_prev, c, h),
         )
 
     def send_up(h, carry):
@@ -216,11 +220,13 @@
 
         lax.fori_loop(0, count, step, 0)
 
-    def keys_left(chip, carry):
+    def key_left(chip):
         gather_copy(k, kbuf, k_send, k_recv, chip, at_chip(chip)).wait_send()
-        return carry
-
-    lax.fori_loop(x + 1, chips, keys_left, 0)
+
+    @pl.when(x > 0)
+    def _():
+        later_chips(key_left)
+
     later_chips(send_values)
 
     @pl.when(core == 1)
@@ -270,14 +276,10 @@
         pb[i] = weights.astype(jnp.bfloat16)
         return carry
 
-    lax.fori_loop(0, blocks * tiles, score_step, 0)
-
-    def up_arrived(h, carry):
-        block = og.at[rows_of(h, up_rows)]
-        remote(block, block, up_recv.at[h], up_recv.at[h], sibling).wait_recv()
-        return carry
-
-    lax.fori_loop(0, heads, up_arrived, 0)
+    lax.fori_loop(0, blocks * tiles, score_step, 0, unroll=True)
+
+    all_up = remote(og, og, up_send, up_recv, sibling)
+    all_up.wait_recv()
 
     def block_sums(lhs, rhs, part):
         def step(qb, carry):
@@ -290,19 +292,32 @@
                 part[qb * slots + t] = total[t * BLK:(t + 1) * BLK]
             return carry
 
-        lax.fori_loop(0, blocks, step, 0)
+        lax.fori_loop(0, blocks, step, 0, unroll=True)
 
     def grad_rows(i, carry):
         os[i] = head_rows(og, i // tiles, i % tiles)
         return carry
 
-    lax.fori_loop(0, blocks * tiles, grad_rows, 0)
+    lax.fori_loop(0, blocks * tiles, grad_rows, 0, unroll=True)
     block_sums(pb, os, part_v)
 
+    half = chips // 2
+
+    def farthest_first(count, step):
+        def turn(i, carry):
+            d = half + (1 - 2 * (i % 2)) * ((i + 1) // 2)
+
+            @pl.when(x >= d)
+            def _():
+                step(x - d)
+
+            return carry
+
+        lax.fori_loop(0, count, turn, 0)
+
     def exchange_copy(src, dst, send, recv, chip):
-        return remote(
-            src.at[rows_of(chip, tok)], dst.at[rows_of(chip, tok)], send.at[chip], recv.at[chip], sibling
-        )
+        at = rows_of(chip, tok)
+        return remote(src.at[at], dst.at[at], send.at[chip], recv.at[chip], sibling)
 
     def exchange(part, own, out, landing, send, recv):
         def owner_block(owner, b):
@@ -312,17 +327,15 @@
                 total = total + part[tbl[qb * all_blocks + j]]
             return total
 
-        def step(chip, carry):
+        def step(chip):
             for b in range(blocks):
                 at = rows_of(chip * blocks + b, BLK)
                 out[at, :] = owner_block(chip * 2 + 1 - core, b).astype(jnp.bfloat16)
             exchange_copy(out, landing, send, recv, chip).start()
             for b in range(blocks):
-                at = rows_of(chip * blocks + b, BLK)
-                own[at, :] = owner_block(chip * 2 + core, b)
-            return carry
-
-        lax.fori_loop(0, x + 1, step, 0)
+                own[rows_of(chip * blocks + b, BLK), :] = owner_block(chip * 2 + core, b)
+
+        farthest_first(chips, step)
 
     exchange(part_v, av, sbv, rbv, ev_send, ev_recv)
 
@@ -346,7 +359,7 @@
             out[at, :] = (own[at, :] + landing[at, :].astype(jnp.float32)).astype(jnp.bfloat16)
             owner_copy(out, owners, rsend, rrecv, chip).start()
 
-        earlier_chips(step, near_first[::-1])
+        farthest_first(chips - 1, step)
         at = rows_of(x, tok)
         exchange_copy(src, landing, send, landed, x).wait_recv()
         own[at, :] = own[at, :] + landing[at, :].astype(jnp.float32)
@@ -361,7 +374,7 @@
 
 
     wait_sibling(vbuf, v_sib, x + 1)
-    lax.fori_loop(0, blocks * tiles, score_grad_step, 0)
+    lax.fori_loop(0, blocks * tiles, score_grad_step, 0, unroll=True)
     block_sums(dsb, qs, part_k)
     exchange(part_k, ak, sbk, rbk, ek_send, ek_recv)
 
@@ -373,11 +386,34 @@
             dq[rows_of(qb, BLK), rows_of(tile * TILE_HEADS + h, HD)] = grad[h * BLK:(h + 1) * BLK]
         return carry
 
-    lax.fori_loop(0, blocks * tiles, query_step, 0)
+    lax.fori_loop(0, blocks * tiles, query_step, 0, unroll=True)
     dq_copy = pltpu.make_async_copy(dq, dq_out.at[0], loc_sem.at[4])
     dq_copy.start()
     send_owned(ak, sbk, rbk, gk, hk, ek_send, ek_recv, rk_send, rk_recv)
 
+    def left_gather(chip, carry):
+        @pl.when(jnp.logical_or(chip == x, x == 0))
+        def _():
+            gather_copy(k, kbuf, k_send, k_recv, chip, at_chip(chip)).wait_send()
+
+        gather_copy(v, vbuf, v_send, v_recv, chip, at_chip(chip)).wait_send()
+        return carry
+
+    def left_lower(chip, carry):
+        passed_on(kbuf, k_fwd, k_sib, chip).wait_send()
+        passed_on(vbuf, v_fwd, v_sib, chip).wait_send()
+        owner_copy(gv, hv, rv_send, rv_recv, chip).wait_send()
+        return carry
+
+    def left_exchange(chip, carry):
+        exchange_copy(sbv, rbv, ev_send, ev_recv, chip).wait_send()
+        exchange_copy(sbk, rbk, ek_send, ek_recv, chip).wait_send()
+        return carry
+
+    lax.fori_loop(x, chips, left_gather, 0)
+    all_up.wait_send()
+    lax.fori_loop(0, x, left_lower, 0)
+    lax.fori_loop(0, x + 1, left_exchange, 0)
     def owned_total(own, landing, recv, at):
         own_rows = own[rows_of(x, tok), :]
 
@@ -395,43 +431,33 @@
     dk_copy = pltpu.make_async_copy(dkv.at[1], dk_out.at[0], loc_sem.at[6])
     dk_copy.start()
 
-    def left_gather(chip, carry):
-        @pl.when(chip == x)
-        def _():
-            gather_copy(k, kbuf, k_send, k_recv, chip, at_chip(chip)).wait_send()
-
-        gather_copy(v, vbuf, v_send, v_recv, chip, at_chip(chip)).wait_send()
-        return carry
-
-    def left_up(h, carry):
-        up_copy(h).wait_send()
-        return carry
-
-    def left_lower(chip, carry):
-        passed_on(kbuf, k_fwd, k_sib, chip).wait_send()
-        passed_on(vbuf, v_fwd, v_sib, chip).wait_send()
-        owner_copy(gv, hv, rv_send, rv_recv, chip).wait_send()
+    def left_owner_keys(chip, carry):
         owner_copy(gk, hk, rk_send, rk_recv, chip).wait_send()
         return carry
 
-    def left_exchange(chip, carry):
-        exchange_copy(sbv, rbv, ev_send, ev_recv, chip).wait_send()
-        exchange_copy(sbk, rbk, ek_send, ek_recv, chip).wait_send()
-        return carry
-
-    lax.fori_loop(x, chips, left_gather, 0)
-    lax.fori_loop(0, heads, left_up, 0)
-    lax.fori_loop(0, x, left_lower, 0)
-    lax.fori_loop(0, x + 1, left_exchange, 0)
+    lax.fori_loop(0, x, left_owner_keys, 0)
     dq_copy.wait()
     dv_copy.wait()
     dk_copy.wait()
 
 
-def hand_on(dq_in, dk_in, dv_in, dq_out, dk_out, dv_out):
-    dq_out[...] = dq_in[...]
-    dk_out[...] = dk_in[...]
-    dv_out[...] = dv_in[...]
+def hand_on(dq_in, dk_in, dv_in, dq_out, dk_out, dv_out, dq, dk, dv, in_sems, out_sems):
+    held = (dq, dk, dv)
+    arriving = [
+        pltpu.make_async_copy(a, b, in_sems.at[i])
+        for i, (a, b) in enumerate(zip((dq_in, dk_in, dv_in), held))
+    ]
+    leaving = [
+        pltpu.make_async_copy(a, b, out_sems.at[i])
+        for i, (a, b) in enumerate(zip(held, (dq_out, dk_out, dv_out)))
+    ]
+    for copy in arriving:
+        copy.start()
+    for there, back in zip(arriving, leaving):
+        there.wait()
+        back.start()
+    for copy in leaving:
+        copy.wait()
 
 
 def per_device(pipes, ctxs, heads, queries, key_states, value_states, upstream, selected):
@@ -464,7 +490,7 @@
         pltpu.SMEM((1, 1, blocks, topb), jnp.int32),
         pltpu.SMEM((blocks * ctxs * blocks,), jnp.int32),
         pltpu.SemaphoreType.REGULAR,
-        dma((7,)), dma((heads,)), dma((heads,)),
+        dma((7,)), dma, dma,
     ] + [dma((chips,)) for _ in range(16)]
     sizes = (pipes, ctxs, heads, tok, topb)
     hbm = pl.BlockSpec(memory_space=pltpu.HBM)
@@ -490,12 +516,13 @@
         value_states.reshape(blocks, BLK, HD),
         upstream,
     )
-    whole = pl.BlockSpec(memory_space=pltpu.VMEM)
     return pl.pallas_call(
         hand_on,
         out_shape=results,
-        in_specs=[whole] * 3,
-        out_specs=(whole, whole, whole),
+        in_specs=[hbm] * 3,
+        out_specs=(hbm, hbm, hbm),
+        scratch_shapes=[vmem(r.shape, r.dtype) for r in results] + [dma((3,)), dma((3,))],
+        compiler_params=pltpu.CompilerParams(vmem_limit_bytes=60 * 1024 * 1024),
         name="hand_on_grads",
     )(*grads)
 

time: 43.9 us -> 42.6 us (0.970)
  Pallas kernels: 43.1 us -> 41.8 us
    pallas_call x1, Pallas kernels: 41.4 us -> 40.1 us  [per_device(): pl.pallas_call(functools.partial(body, sizes), out_shape=results, in_spec...]
where the time goes in v5:
time: 42.6 us; the launch traced here: 42.4 us
  Pallas kernels  41.8 us (98%)
  between operations  0.64 us (2%)
    pallas_call x1, Pallas kernels, per_device(): pl.pallas_call(functools.partial(body, sizes), out_shape=results, in_spec...  40.1 us
    pallas_call x1, Pallas kernels, per_device(): pl.pallas_call(hand_on, out_shape=results, in_specs=[hbm] * 3, out_specs=...  1.71 us

profile of v5, /device:TPU:1, one launch (start us, length us, event | category | flops | bytes accessed | tf_op | source)
XLA Modules:
  0.0 42.4 jit_solution(14113933339273108989)
XLA Ops:
  0.6 40.1 %selected_attention_grads.1 = (bf16[1,128,1024]{2,1,0:T(8,128)(2,1)}, bf16[1,128,128]{2,1,0:T(8,128)(2,1)}, bf16[1,128,128]{2,1,0:T(8,128)(2,1)}) custom-call(s32[1,1,2,8]{3,2,1,0:T(2,128)} %sel_in.1, bf16[1,128,1024]{2,1,0:T(8,128)(2,1)} %q.1, bf16[2,64,128]{2,1,0:T(8,128)(2,1)} %bitcast.2, bf16[2,64,128]{2,1,0:T(8,128)(2,1)} %bitcast.3, ...), custom_call_target="tpu_custom_call" | custom-call | tf_op jit(solution)/shard_map/selected_attention_grads/pallas_call | solution.py:502
  40.7 1.7 %hand_on_grads.1 = (bf16[1,128,1024]{2,1,0:T(8,128)(2,1)}, bf16[1,128,128]{2,1,0:T(8,128)(2,1)}, bf16[1,128,128]{2,1,0:T(8,128)(2,1)}) custom-call(bf16[1,128,1024]{2,1,0:T(8,128)(2,1)} %get-tuple-element.6.dq_in, bf16[1,128,128]{2,1,0:T(8,128)(2,1)} %get-tuple-element.7.dk_in, bf16[1,128,128]{2,1,0:T(8,128)(2,1)} %get-tuple-element.8.dv_in), custom_call_target="tpu_custom_call" | custom-call | tf_op jit(solution)/shard_map/hand_on_grads/pallas_call | solution.py:519

commit v6 on v5

--- a/solution.py
+++ b/solution.py
@@ -26,7 +26,7 @@
     pipes, ctxs, heads, tok, topb = sizes
     (
         kbuf, vbuf, qv, og, qs, os, ks, pf, pb, dsb, part_v, part_k,
-        av, ak, sbv, sbk, rbv, rbk, gv, gk, hv, hk, dq, dkv, sel, tbl, ready,
+        av, ak, sbv, sbk, rbv, rbk, gv, gk, hv, hk, sel, tbl, ready,
         loc_sem, up_send, up_recv,
         k_send, k_recv, k_fwd, k_sib, v_send, v_recv, v_fwd, v_sib,
         ev_send, ev_recv, ek_send, ek_recv,
@@ -383,12 +383,10 @@
         grad = lax.dot_general(dsb[i], ks[qb], TN_DIMS, preferred_element_type=jnp.float32)
         grad = grad.astype(jnp.bfloat16)
         for h in range(TILE_HEADS):
-            dq[rows_of(qb, BLK), rows_of(tile * TILE_HEADS + h, HD)] = grad[h * BLK:(h + 1) * BLK]
+            dq_out[0, rows_of(qb, BLK), rows_of(tile * TILE_HEADS + h, HD)] = grad[h * BLK:(h + 1) * BLK]
         return carry
 
     lax.fori_loop(0, blocks * tiles, query_step, 0, unroll=True)
-    dq_copy = pltpu.make_async_copy(dq, dq_out.at[0], loc_sem.at[4])
-    dq_copy.start()
     send_owned(ak, sbk, rbk, gk, hk, ek_send, ek_recv, rk_send, rk_recv)
 
     def left_gather(chip, carry):
@@ -414,7 +412,7 @@
     all_up.wait_send()
     lax.fori_loop(0, x, left_lower, 0)
     lax.fori_loop(0, x + 1, left_exchange, 0)
-    def owned_total(own, landing, recv, at):
+    def owned_total(own, landing, recv, out):
         own_rows = own[rows_of(x, tok), :]
 
         def step(chip, total):
@@ -422,41 +420,24 @@
             remote(block, block, recv.at[chip], recv.at[chip], sibling).wait_recv()
             return total + landing[chip].astype(jnp.float32)
 
-        dkv[at] = lax.fori_loop(x + 1, chips, step, own_rows).astype(jnp.bfloat16)
-
-    owned_total(av, hv, rv_recv, 0)
-    dv_copy = pltpu.make_async_copy(dkv.at[0], dv_out.at[0], loc_sem.at[5])
-    dv_copy.start()
-    owned_total(ak, hk, rk_recv, 1)
-    dk_copy = pltpu.make_async_copy(dkv.at[1], dk_out.at[0], loc_sem.at[6])
-    dk_copy.start()
+        out[0] = lax.fori_loop(x + 1, chips, step, own_rows).astype(jnp.bfloat16)
+
+    owned_total(av, hv, rv_recv, dv_out)
+    owned_total(ak, hk, rk_recv, dk_out)
 
     def left_owner_keys(chip, carry):
         owner_copy(gk, hk, rk_send, rk_recv, chip).wait_send()
         return carry
 
     lax.fori_loop(0, x, left_owner_keys, 0)
-    dq_copy.wait()
-    dv_copy.wait()
-    dk_copy.wait()
-
-
-def hand_on(dq_in, dk_in, dv_in, dq_out, dk_out, dv_out, dq, dk, dv, in_sems, out_sems):
-    held = (dq, dk, dv)
-    arriving = [
-        pltpu.make_async_copy(a, b, in_sems.at[i])
-        for i, (a, b) in enumerate(zip((dq_in, dk_in, dv_in), held))
-    ]
-    leaving = [
-        pltpu.make_async_copy(a, b, out_sems.at[i])
-        for i, (a, b) in enumerate(zip(held, (dq_out, dk_out, dv_out)))
-    ]
-    for copy in arriving:
+
+
+def hand_on(dq_in, dk_in, dv_in, dq_out, dk_out, dv_out, sems):
+    pairs = ((dq_in, dq_out), (dk_in, dk_out), (dv_in, dv_out))
+    copies = [pltpu.make_async_copy(a, b, sems.at[i]) for i, (a, b) in enumerate(pairs)]
+    for copy in copies:
         copy.start()
-    for there, back in zip(arriving, leaving):
-        there.wait()
-        back.start()
-    for copy in leaving:
+    for copy in copies:
         copy.wait()
 
 
@@ -486,7 +467,6 @@
         vmem(owned, bf16), vmem(owned, bf16), vmem(owned, bf16), vmem(owned, bf16),
         vmem(owned, bf16), vmem(owned, bf16),
         vmem((chips, tok, HD), bf16), vmem((chips, tok, HD), bf16),
-        vmem((tok, width), bf16), vmem((2, tok, HD), bf16),
         pltpu.SMEM((1, 1, blocks, topb), jnp.int32),
         pltpu.SMEM((blocks * ctxs * blocks,), jnp.int32),
         pltpu.SemaphoreType.REGULAR,
@@ -494,6 +474,7 @@
     ] + [dma((chips,)) for _ in range(16)]
     sizes = (pipes, ctxs, heads, tok, topb)
     hbm = pl.BlockSpec(memory_space=pltpu.HBM)
+    whole = pl.BlockSpec(memory_space=pltpu.VMEM)
     results = (
         jax.ShapeDtypeStruct(queries.shape, bf16),
         jax.ShapeDtypeStruct(key_states.shape, bf16),
@@ -501,9 +482,9 @@
     )
     grads = pl.pallas_call(
         functools.partial(body, sizes),
-        out_shape=results,
+        out_shape=tuple(vmem(r.shape, r.dtype) for r in results),
         in_specs=[hbm] * 5,
-        out_specs=(hbm, hbm, hbm),
+        out_specs=(whole, whole, whole),
         scratch_shapes=scratch,
         compiler_params=pltpu.CompilerParams(
             collective_id=0, has_side_effects=True, vmem_limit_bytes=60 * 1024 * 1024
@@ -519,12 +500,12 @@
     return pl.pallas_call(
         hand_on,
         out_shape=results,
-        in_specs=[hbm] * 3,
+        in_specs=[whole] * 3,
         out_specs=(hbm, hbm, hbm),
-        scratch_shapes=[vmem(r.shape, r.dtype) for r in results] + [dma((3,)), dma((3,))],
+        scratch_shapes=[dma((3,))],
         compiler_params=pltpu.CompilerParams(vmem_limit_bytes=60 * 1024 * 1024),
         name="hand_on_grads",
-    )(*grads)
+    )(*[pltpu.with_memory_space_constraint(g, pltpu.VMEM) for g in grads])
 
 
 def solution(mesh):

time: 42.6 us -> 41 us (0.962)
  Pallas kernels: 41.8 us -> 40.2 us
    pallas_call x2, Pallas kernels: 41.8 us -> 40.2 us  [the longest x1 39.5 us: per_device(): pl.pallas_call(functools.partial(body, sizes), out_shape=tuple((vmem(r.sh...]
where the time goes in v6:
time: 41 us; the launch traced here: 40.8 us
  Pallas kernels  40.2 us (98%)
  between operations  0.64 us (2%)
    pallas_call x1, Pallas kernels, per_device(): pl.pallas_call(functools.partial(body, sizes), out_shape=tuple((vmem(r.sh...  39.5 us

profile of v6, /device:TPU:1, one launch (start us, length us, event | category | flops | bytes accessed | tf_op | source)
XLA Modules:
  0.0 40.8 jit_solution(11398754858220581601)
XLA Ops:
  0.6 39.5 %selected_attention_grads.1 = (bf16[1,128,1024]{2,1,0:T(8,128)(2,1)S(1)}, bf16[1,128,128]{2,1,0:T(8,128)(2,1)S(1)}, bf16[1,128,128]{2,1,0:T(8,128)(2,1)S(1)}) custom-call(s32[1,1,2,8]{3,2,1,0:T(2,128)} %sel_in.1, bf16[1,128,1024]{2,1,0:T(8,128)(2,1)} %q.1, bf16[2,64,128]{2,1,0:T(8,128)(2,1)} %bitcast.2, bf16[2,64,128]{2,1,0:T(8,128)(2,1)} %bitcast.3, ...), custom_call_target="tpu_custom_call" | custom-call | tf_op jit(solution)/shard_map/selected_attention_grads/pallas_call | solution.py:483
  40.1 0.7 %hand_on_grads.1 = (bf16[1,128,1024]{2,1,0:T(8,128)(2,1)}, bf16[1,128,128]{2,1,0:T(8,128)(2,1)}, bf16[1,128,128]{2,1,0:T(8,128)(2,1)}) custom-call(bf16[1,128,1024]{2,1,0:T(8,128)(2,1)S(1)} %get-tuple-element.6.dq_in, bf16[1,128,128]{2,1,0:T(8,128)(2,1)S(1)} %get-tuple-element.7.dk_in, bf16[1,128,128]{2,1,0:T(8,128)(2,1)S(1)} %get-tuple-element.8.dv_in), custom_call_target="tpu_custom_call" | custom-call | tf_op jit(solution)/shard_map/hand_on_grads/pallas_call | solution.py:500

commit v7 on v6

--- a/solution.py
+++ b/solution.py
@@ -386,8 +386,8 @@
             dq_out[0, rows_of(qb, BLK), rows_of(tile * TILE_HEADS + h, HD)] = grad[h * BLK:(h + 1) * BLK]
         return carry
 
+    send_owned(ak, sbk, rbk, gk, hk, ek_send, ek_recv, rk_send, rk_recv)
     lax.fori_loop(0, blocks * tiles, query_step, 0, unroll=True)
-    send_owned(ak, sbk, rbk, gk, hk, ek_send, ek_recv, rk_send, rk_recv)
 
     def left_gather(chip, carry):
         @pl.when(jnp.logical_or(chip == x, x == 0))

time: 41 us -> 40.7 us (level)
  no operation moved by 1% of the time
where the time goes in v7:
time: 40.7 us; the launch traced here: 40.5 us
  Pallas kernels  39.9 us (98%)
  between operations  0.64 us (2%)
    pallas_call x1, Pallas kernels, per_device(): pl.pallas_call(functools.partial(body, sizes), out_shape=tuple((vmem(r.sh...  39.2 us

profile of v7, /device:TPU:1, one launch (start us, length us, event | category | flops | bytes accessed | tf_op | source)
XLA Modules:
  0.0 40.5 jit_solution(5246300997676325581)
XLA Ops:
  0.6 39.2 %selected_attention_grads.1 = (bf16[1,128,1024]{2,1,0:T(8,128)(2,1)S(1)}, bf16[1,128,128]{2,1,0:T(8,128)(2,1)S(1)}, bf16[1,128,128]{2,1,0:T(8,128)(2,1)S(1)}) custom-call(s32[1,1,2,8]{3,2,1,0:T(2,128)} %sel_in.1, bf16[1,128,1024]{2,1,0:T(8,128)(2,1)} %q.1, bf16[2,64,128]{2,1,0:T(8,128)(2,1)} %bitcast.2, bf16[2,64,128]{2,1,0:T(8,128)(2,1)} %bitcast.3, ...), custom_call_target="tpu_custom_call" | custom-call | tf_op jit(solution)/shard_map/selected_attention_grads/pallas_call | solution.py:483
  39.8 0.7 %hand_on_grads.1 = (bf16[1,128,1024]{2,1,0:T(8,128)(2,1)}, bf16[1,128,128]{2,1,0:T(8,128)(2,1)}, bf16[1,128,128]{2,1,0:T(8,128)(2,1)}) custom-call(bf16[1,128,1024]{2,1,0:T(8,128)(2,1)S(1)} %get-tuple-element.6.dq_in, bf16[1,128,128]{2,1,0:T(8,128)(2,1)S(1)} %get-tuple-element.7.dk_in, bf16[1,128,128]{2,1,0:T(8,128)(2,1)S(1)} %get-tuple-element.8.dv_in), custom_call_target="tpu_custom_call" | custom-call | tf_op jit(solution)/shard_map/hand_on_grads/pallas_call | solution.py:500
